TPU v7x, 128 devices: a whole 4x4x4 slice. The times are simulated.
128 devices in a mesh: dp: 4 (over y), ctx: 32 (over z, x, core).
Axes of the slice: x: 4, y: 4, z: 4, core: 2. Of those that a mesh axis runs over, the one named last changes fastest.
Arguments:
- projected: bfloat16 [4, 4096, 3, 8192], P('dp', 'ctx'), may hold values from -6 to 6
- short_filter: float32 [3, 7, 8192], replicated, may hold values from -2.4 to 2.4
- residues: float32 [512, 16], replicated, may hold values from -0.06 to 0.06
- decay_rates: float32 [512, 16], replicated, may hold values from 2.4414063e-05 to 0.03125
- skip_gain: float32 [8192], replicated, may hold values from 0.5 to 1.5
- cotangent: bfloat16 [4, 4096, 8192], P('dp', 'ctx'), may hold values from -6 to 6
Outputs:
- output: bfloat16 [4, 4096, 8192], P('dp', 'ctx')
- grad_projected: bfloat16 [4, 4096, 3, 8192], P('dp', 'ctx')
- grad_short: float32 [3, 7, 8192], replicated
- grad_skip: float32 [8192], replicated
All inputs are finite; a program needn't handle non-finite values.
Results may differ from a plain program's by a relative error of at most 0.001.
Values may be sent and summed in bfloat16 or wider, within the bound.
A program may use at most 320 MiB of HBM per device.

v0:
```python
import jax
import jax.numpy as jnp
from jax import lax
from jax.sharding import PartitionSpec as P

BLK = 64


HIGHEST = lax.Precision.HIGHEST


def passed_along(value, axis, steps):
    count = lax.axis_size(axis)
    first, last = (max(0, -steps), min(count, count - steps))
    return lax.ppermute(value, axis, [(source, source + steps) for source in range(first, last)])


def edge_tables(residues, decay_rates, span):
    offsets = jnp.arange(span).astype(jnp.float32)
    carry_fwd = residues[:, None, :] * jnp.exp(
        -decay_rates[:, None, :] * (offsets[None, :, None] + 1.0)
    )
    carry_bwd = residues[:, None, :] * jnp.exp(
        -decay_rates[:, None, :] * (span - offsets)[None, :, None]
    )
    decay_factor = jnp.exp(-decay_rates * span)
    return (carry_fwd, carry_bwd, decay_factor)


def block_tables(residues, decay_rates, block_rows):
    offsets = jnp.arange(block_rows).astype(jnp.float32)
    powers = jnp.exp(-decay_rates[:, :, None] * offsets[None, None, :])
    lag_filter = jnp.sum(residues[:, :, None] * powers, axis=1)
    lag_index = jnp.arange(block_rows)[:, None] - jnp.arange(block_rows)[None, :]
    toeplitz = jnp.where(lag_index >= 0, lag_filter[:, jnp.maximum(lag_index, 0)], 0.0)
    carry_fwd, carry_bwd, decay_factor = edge_tables(residues, decay_rates, block_rows)
    return (toeplitz, powers[:, :, ::-1], powers, carry_fwd, carry_bwd, decay_factor)


def forward_local(inputs, tables):
    toeplitz, end_weights, start_weights, carry_fwd, carry_bwd, decay_factor = tables
    local_out = jnp.einsum("gts,bkswg->bktwg", toeplitz, inputs, precision=HIGHEST)
    block_ends = jnp.einsum("gns,bkswg->bknwg", end_weights, inputs, precision=HIGHEST)
    factor = decay_factor.T[:, None, :]

    def forward_advance(carried, block_term):
        return (factor * carried + block_term, carried)

    final_state, entering = lax.scan(
        forward_advance, jnp.zeros_like(block_ends[:, 0]), jnp.moveaxis(block_ends, 1, 0)
    )
    entering = jnp.moveaxis(entering, 0, 1)
    local_out = local_out + jnp.einsum("gjn,bknwg->bkjwg", carry_fwd, entering, precision=HIGHEST)
    return (local_out, final_state)


def backward_local(grads, tables):
    toeplitz, end_weights, start_weights, carry_fwd, carry_bwd, decay_factor = tables
    local_grad = jnp.einsum("gts,bktwg->bkswg", toeplitz, grads, precision=HIGHEST)
    block_starts = jnp.einsum("gnt,bktwg->bknwg", start_weights, grads, precision=HIGHEST)
    factor = decay_factor.T[:, None, :]

    def backward_advance(carried, block_term):
        return (factor * carried + block_term, carried)

    final_adjoint, following = lax.scan(
        backward_advance,
        jnp.zeros_like(block_starts[:, 0]),
        jnp.moveaxis(block_starts, 1, 0),
        reverse=True,
    )
    following = jnp.moveaxis(following, 0, 1)
    local_grad = local_grad + jnp.einsum(
        "gsn,bknwg->bkswg", carry_bwd, following, precision=HIGHEST
    )
    return (local_grad, final_adjoint)


def short_conv(padded, short_filter, count):
    tap_count = short_filter.shape[1]
    total = jnp.zeros((padded.shape[0], count) + padded.shape[2:], jnp.float32)
    for offset in range(tap_count):
        begin = tap_count - 1 - offset
        total = total + short_filter[:, offset, :] * padded[:, begin : begin + count].astype(
            jnp.float32
        )
    return total


def short_conv_grad(ahead, short_filter, count):
    tap_count = short_filter.shape[1]
    total = jnp.zeros((ahead.shape[0], count) + ahead.shape[2:], jnp.float32)
    for offset in range(tap_count):
        total = total + short_filter[:, offset, :] * ahead[:, offset : offset + count]
    return total


def filter_grad(grad_mixed, padded, tap_count, count):
    products = jnp.stack(
        [
            grad_mixed
            * padded[:, tap_count - 1 - offset : tap_count - 1 - offset + count].astype(jnp.float32)
            for offset in range(tap_count)
        ],
        axis=3,
    )
    return jnp.sum(products, axis=(0, 1))


def chains(local_end, local_adjoint, factor):
    wide_factor = factor[:, None, :]

    def forward_turn(turn_index, incoming):
        return passed_along(wide_factor * incoming + local_end, "ctx", 1)

    def backward_turn(turn_index, incoming):
        return passed_along(wide_factor * incoming + local_adjoint, "ctx", -1)

    entering = lax.fori_loop(0, lax.axis_size("ctx") - 1, forward_turn, jnp.zeros_like(local_end))
    arriving = lax.fori_loop(
        0, lax.axis_size("ctx") - 1, backward_turn, jnp.zeros_like(local_adjoint)
    )
    return (entering, arriving)


def local(projected, short_filter, residues, decay_rates, skip_gain, cotangent):
    batch_size = projected.shape[0]
    local_rows = projected.shape[1]
    channels = projected.shape[3]
    tap_count = short_filter.shape[1]
    filter_groups = residues.shape[0]
    group_width = channels // filter_groups
    previous = passed_along(projected[:, local_rows - (tap_count - 1) :], "ctx", 1)
    padded = jnp.concatenate([previous, projected], axis=1)
    mixed = short_conv(padded, short_filter, local_rows)
    query_part = mixed[:, :, 0]
    key_part = mixed[:, :, 1]
    value_part = mixed[:, :, 2]
    gated = key_part * value_part
    tables = block_tables(residues, decay_rates, BLK)
    carry_fwd, carry_bwd, decay_device = edge_tables(residues, decay_rates, local_rows)
    device_factor = decay_device.T
    block_shape = (batch_size, local_rows // BLK, BLK, group_width, filter_groups)
    conv_out, local_end = forward_local(gated.reshape(block_shape), tables)
    upstream = cotangent.astype(jnp.float32)
    grad_filtered = upstream * query_part
    conv_grad, local_adjoint = backward_local(grad_filtered.reshape(block_shape), tables)
    entering, arriving = chains(local_end, local_adjoint, device_factor)
    carried = jnp.einsum("gtn,bnwg->btwg", carry_fwd, entering, precision=HIGHEST)
    filtered = conv_out.reshape(gated.shape) + carried.reshape(gated.shape) + skip_gain * gated
    output = (query_part * filtered).astype(jnp.bfloat16)
    grad_query = upstream * filtered
    returned = jnp.einsum("gsn,bnwg->bswg", carry_bwd, arriving, precision=HIGHEST)
    grad_gated = (
        conv_grad.reshape(gated.shape) + returned.reshape(gated.shape) + skip_gain * grad_filtered
    )
    grad_mixed = jnp.stack([grad_query, grad_gated * value_part, grad_gated * key_part], axis=2)
    following = passed_along(grad_mixed[:, : tap_count - 1], "ctx", -1)
    ahead = jnp.concatenate([grad_mixed, following], axis=1)
    grad_projected = short_conv_grad(ahead, short_filter, local_rows).astype(jnp.bfloat16)
    short_local = filter_grad(grad_mixed, padded, tap_count, local_rows)
    skip_local = jnp.sum(grad_filtered * gated, axis=(0, 1))
    grad_short, grad_skip = lax.psum((short_local, skip_local), ("dp", "ctx"))
    return (output, grad_projected, grad_short, grad_skip)


def solution(mesh):
    placed = (P("dp", "ctx", None, None), P(), P(), P(), P(), P("dp", "ctx", None))
    return jax.shard_map(
        local,
        mesh=mesh,
        in_specs=placed,
        out_specs=(P("dp", "ctx", None), P("dp", "ctx", None, None), P(), P()),
        check_vma=False,
    )
```

profile of v0, /device:TPU:1, one launch (start us, length us, event | category | flops | bytes accessed | tf_op | source)
XLA Modules:
  0.0 1422.1 jit_solution(7022299706834155832)
XLA Ops:
  33.3 16.8 %gather_fusion = f32[4096,512]{1,0:T(8,128)} fusion(f32[512,64]{0,1:T(8,128)S(1)} %copy.52, s32[4096]{0:T(1024)S(1)} %broadcast_clamp_fusion), kind=kCustom, calls=%fused_computation | custom fusion | bytes 16793600 | tf_op jit(solution)/shard_map/gather | solution.py:35
  50.1 16.2 %copy.53 = f32[64,64,512]{1,0,2:T(8,128)} copy(f32[64,64,512]{2,1,0:T(8,128)} %bitcast.190) | data formatting | bytes 16777216 | tf_op jit(solution)/shard_map/gather | solution.py:35
  66.9 18.8 %fusion.11 = f32[1,128,3,8192]{3,1,2,0:T(8,128)S(1)} fusion(bf16[1,128,3,8192]{3,1,2,0:T(8,128)(2,1)} %param.14, bf16[1,6,3,8192]{3,1,2,0:T(8,128)(2,1)S(1)} %collective-permute-done.2, f32[3,8192]{1,0:T(4,128)S(1)} %get-tuple-element.314, f32[3,8192]{1,0:T(4,128)S(1)} %get-tuple-element.315, f32[3,8192]{1,0:T(4,128)S(1)} %get-tuple-element.316, ...), kind=kLoop, calls=%fused_computation.38 | loop fusion | flops 119537664 | bytes 19857408 | tf_op jit(solution)/shard_map/add | solution.py:84
  101.1 13.1 fusion.67
  127.8 29.5 %fusion.2 = f32[512,2,16,64]{3,2,1,0:T(8,128)S(1)} fusion(f32[2,64,16,512]{1,2,0,3:T(8,128)} %copy.54, f32[64,64,512]{1,0,2:T(8,128)} %copy.53, pred[64,64]{1,0:T(8,128)(4,1)S(1)} %subtract_compare_fusion), kind=kOutput, calls=%fused_computation.9 | convolution fusion | flops 807403520 | bytes 16781312 | tf_op jit(solution)/shard_map/gts,bkswg->bktwg/dot_general | solution.py:42
  157.3 11.3 add_bitcast_fusion.1
  181.3 353.5 %while.50 = (s32[]{:T(128)}, f32[1,16,16,512]{3,2,1,0:T(8,128)S(1)}, f32[16,512]{1,0:T(8,128)S(1)}, f32[1,16,16,512]{3,2,1,0:T(8,128)S(1)}, s32[]{:T(128)}) while((s32[]{:T(128)}, f32[1,16,16,512]{3,2,1,0:T(8,128)S(1)}, f32[16,512]{1,0:T(8,128)S(1)}, f32[1,16,16,512]{3,2,1,0:T(8,128)S(1)}, s32[]{:T(128)}) %tuple.113), condition=%wide.region_4.5_spmd, body=%wide.region_3.4_spmd.sunk | while | flops 262146 | bytes 3702885 | solution.py:119
  555.1 13.5 multiply_reduce_fusion
  584.9 12.2 fusion.72
  597.1 19.1 %fusion = f32[512,2,16,64]{3,2,1,0:T(8,128)} fusion(f32[2,64,16,512]{1,2,0,3:T(8,128)S(1)} %copy-done.5, f32[64,64,512]{1,0,2:T(8,128)} %copy.53, pred[64,64]{1,0:T(8,128)(4,1)S(1)} %subtract_compare_fusion), kind=kOutput, calls=%fused_computation.7 | convolution fusion | flops 807403520 | bytes 16781312 | tf_op jit(solution)/shard_map/gts,bktwg->bkswg/dot_general | solution.py:59
  630.3 13.7 add_bitcast_fusion
  656.7 397.2 %while.51 = (s32[]{:T(128)}, f32[1,16,16,512]{3,2,1,0:T(8,128)S(1)}, f32[16,512]{1,0:T(8,128)S(1)}, f32[1,16,16,512]{3,2,1,0:T(8,128)S(1)}, s32[]{:T(128)}) while((s32[]{:T(128)}, f32[1,16,16,512]{3,2,1,0:T(8,128)S(1)}, f32[16,512]{1,0:T(8,128)S(1)}, f32[1,16,16,512]{3,2,1,0:T(8,128)S(1)}, s32[]{:T(128)}) %tuple.125), condition=%wide.region_8.9_spmd, body=%wide.region_7.8_spmd.sunk | while | flops 262146 | bytes 3702885 | solution.py:120
  658.8 11.4 collective-permute-done.1
  684.8 11.4 collective-permute-done.1
  710.9 11.4 collective-permute-done.1
  737.0 11.4 collective-permute-done.1
  750.5 10.7 collective-permute-done.1
  775.9 10.7 collective-permute-done.1
  801.4 10.7 collective-permute-done.1
  839.6 10.7 collective-permute-done.1
  865.0 10.7 collective-permute-done.1
  903.2 10.7 collective-permute-done.1
  928.7 10.7 collective-permute-done.1
  954.1 10.7 collective-permute-done.1
  992.3 10.7 collective-permute-done.1
  1074.3 10.8 fusion.51
  1094.9 10.9 fusion.13
  1119.3 11.2 fusion.15
  1157.5 27.9 %reduce_sum.28 = f32[3,7,8192]{2,0,1:T(4,128)} reduce(f32[1,128,3,7,8192]{4,1,2,3,0:T(8,128)} %fusion.25, f32[]{:T(128)} %constant.65.clone.1), dimensions={0,1}, to_apply=%region_9.10 | reduce | flops 21848064 | bytes 88768512 | tf_op jit(solution)/shard_map/reduce_sum | solution.py:107
  1185.5 102.3 %psum.15 = f32[8192]{0:T(1024)} all-reduce(f32[8192]{0:T(1024)S(1)} %copy-done.25), channel_id=1, replica_groups=mesh['dp'=4,'ctx'=32] {'dp','ctx'}, use_global_device_ids=true, to_apply=%region_12.13 | all-reduce | flops 8192 | bytes 65536 | tf_op jit(solution)/shard_map/psum | solution.py:163
  1287.8 80.9 %all-reduce.2.cloned.1.call-done = f32[3,7,8192]{2,0,1:T(4,128)} async-done(((f32[3,7,8192]{2,0,1:T(4,128)}), f32[3,7,8192]{2,0,1:T(4,128)}) %all-reduce.2.cloned.1.call-update) | async-done | bytes 688144 | tf_op jit(solution)/shard_map/psum | solution.py:163
  1381.5 33.6 %fusion.27 = bf16[1,128,3,8192]{3,1,2,0:T(8,128)(2,1)} fusion(f32[1,134,3,8192]{3,1,2,0:T(8,128)} %pad_maximum_fusion, f32[3,8192]{1,0:T(4,128)S(1)} %copy-done.13, f32[3,8192]{1,0:T(4,128)S(1)} %copy-done.15, f32[3,8192]{1,0:T(4,128)S(1)} %copy-done.17, f32[3,8192]{1,0:T(4,128)S(1)} %copy-done.19, f32[3,8192]{1,0:T(4,128)S(1)} %copy-done.21, ...), kind=kLoop, calls=%fused_computation.55 | loop fusion | flops 50331648 | bytes 95059968 | tf_op jit(solution)/shard_map/convert_element_type | solution.py:160
  (306 shorter events, 823.4 us)
Async XLA Ops:
  7.2 1361.6 %all-reduce.2.cloned.1.call-start = ((), (), s32[]{:S(2)}) async-start(), calls=%async_computation | async-start | bytes 1835008 | tf_op jit(solution)/shard_map/psum | solution.py:163
  8.3 58.6 %collective-permute-start.2 = (bf16[1,6,3,8192]{3,1,2,0:T(8,128)(2,1)S(1)}, bf16[1,6,3,8192]{3,1,2,0:T(8,128)(2,1)S(1)}, u32[]{:S(2)}, u32[]{:S(2)}) collective-permute-start(bf16[1,6,3,8192]{3,1,2,0:T(8,128)(2,1)S(1)} %slice.87), channel_id=1, source_target_pairs={{0,1},{1,2},{2,3},{3,4},{4,5},{5,6},{6,7},{7,8},{8,9},{9,10},{10,1... | collective-permute-start | bytes 884744 | tf_op jit(solution)/shard_map/ppermute | solution.py:15
  382.2 12.6 collective-permute-start
  395.0 12.6 collective-permute-start
  407.7 12.6 collective-permute-start
  420.4 12.6 collective-permute-start
  433.1 12.6 collective-permute-start
  445.9 12.6 collective-permute-start
  458.6 12.6 collective-permute-start
  471.3 12.6 collective-permute-start
  484.1 12.6 collective-permute-start
  496.8 12.6 collective-permute-start
  509.5 12.6 collective-permute-start
  522.2 12.6 collective-permute-start
  656.8 13.4 collective-permute-start.1
  682.9 13.4 collective-permute-start.1
  709.0 13.4 collective-permute-start.1
  735.1 13.4 collective-permute-start.1
  748.5 12.6 collective-permute-start.1
  774.0 12.6 collective-permute-start.1
  786.7 12.6 collective-permute-start.1
  799.5 12.6 collective-permute-start.1
  812.2 12.6 collective-permute-start.1
  837.6 12.6 collective-permute-start.1
  863.1 12.6 collective-permute-start.1
  875.8 12.6 collective-permute-start.1
  901.3 12.6 collective-permute-start.1
  926.7 12.6 collective-permute-start.1
  939.5 12.6 collective-permute-start.1
  952.2 12.6 collective-permute-start.1
  964.9 12.6 collective-permute-start.1
  1117.0 254.2 %collective-permute-start.3 = (f32[1,6,3,8192]{3,0,2,1:T(1,128)S(1)}, f32[1,6,3,8192]{3,0,2,1:T(1,128)S(1)}, u32[]{:S(2)}, u32[]{:S(2)}) collective-permute-start(f32[1,6,3,8192]{3,0,2,1:T(1,128)S(1)} %copy.74), channel_id=1, source_target_pairs={{1,0},{2,1},{3,2},{4,3},{5,4},{6,5},{7,6},{8,7},{9,8},{10,9},{11,1... | collective-permute-start | bytes 1769480 | tf_op jit(solution)/shard_map/ppermute | solution.py:15
  (61 other events, 797.8 us)
Sparse Core Ops, SparseCore 0:
  1185.6 183.0 all-reduce.1
where the time goes:
time: 1430 us; the launch traced here: 1420 us
  waiting for transfers between devices  604 us (42%)
  starting transfers between devices  227 us (16%)
  other arithmetic  199 us (14%)
  local copies, waits for them, and re-layouts  160 us (11%)
  matrix products  114 us (8%)
  blocking collectives  102 us (7%)
  between operations  14.9 us (1%)
    ppermute x64, waiting for transfers between devices, passed_along(): lax.ppermute(value, axis, [(source, source + steps) for source in range(f...  523 us
    ppermute x64, starting transfers between devices, passed_along(): lax.ppermute(value, axis, [(source, source + steps) for source in range(f...  227 us
    psum x1, blocking collectives, local(): grad_short, grad_skip = lax.psum((short_local, skip_local), ('dp', 'ctx'))  102 us
    psum x1, waiting for transfers between devices, local(): grad_short, grad_skip = lax.psum((short_local, skip_local), ('dp', 'ctx'))  80.9 us
    unnamed x9, other arithmetic  43.6 us
    convert_element_type x1, other arithmetic, local(): short_conv_grad(ahead, short_filter, local_rows).astype(jnp.bfloat16)  33.6 us
    gather x2, local copies, waits for them, and re-layouts, block_tables(): lag_filter[:, jnp.maximum(lag_index, 0)]  33.1 us
    another operation x9, local copies, waits for them, and re-layouts  32 us
  transfers between devices with their start and end apart: 65, of which 63 were waited for; matrix products, arithmetic and copies ran while one was open for 9% of the time, Pallas kernels for 0%

commit v1 on v0

v1 whole, which is shorter than its diff:
```python
import functools
import jax
import jax.numpy as jnp
from jax import lax
from jax.experimental import pallas as pl
from jax.experimental.pallas import tpu as pltpu
from jax.sharding import PartitionSpec as P

MESH = pl.DeviceIdType.MESH
F32 = jnp.float32
ROWS = 128
HALO = 8
EXT = ROWS + HALO
TILES = 8
POLES = 16
TAPS = 7
CHIPS = 16
GRADS = 24


def halo_kernel(proj, cot, prev, nextp, nextc, send_sem, recv_sem):
    dp, me = lax.axis_index("dp"), lax.axis_index("ctx")
    count = lax.axis_size("ctx")
    up, down = lax.rem(me + 1, count), lax.rem(me + count - 1, count)
    barrier = pltpu.get_barrier_semaphore()
    for other in (up, down):
        pl.semaphore_signal(barrier, inc=1, device_id=(dp, other), device_id_type=MESH)
    pl.semaphore_wait(barrier, 2)
    last, first = pl.ds(ROWS - HALO, HALO), pl.ds(0, HALO)
    moves = (
        (proj.at[:, last, :], prev, up),
        (proj.at[:, first, :], nextp, down),
        (cot.at[first, :], nextc, down),
    )
    copies = [
        pltpu.make_async_remote_copy(
            src_ref=source,
            dst_ref=target,
            send_sem=send_sem.at[k],
            recv_sem=recv_sem.at[k],
            device_id=(dp, other),
            device_id_type=MESH,
        )
        for k, (source, target, other) in enumerate(moves)
    ]
    for copy in copies:
        copy.start()
    for copy in copies:
        copy.wait()


def halo(proj, cot):
    channels = proj.shape[2]
    anywhere = pl.BlockSpec(memory_space=pl.ANY)
    return pl.pallas_call(
        halo_kernel,
        name="halo",
        out_shape=(
            jax.ShapeDtypeStruct((3, HALO, channels), proj.dtype),
            jax.ShapeDtypeStruct((3, HALO, channels), proj.dtype),
            jax.ShapeDtypeStruct((HALO, channels), proj.dtype),
        ),
        in_specs=[anywhere, anywhere],
        out_specs=(anywhere, anywhere, anywhere),
        scratch_shapes=[pltpu.SemaphoreType.DMA((3,)), pltpu.SemaphoreType.DMA((3,))],
        compiler_params=pltpu.CompilerParams(collective_id=0, has_side_effects=True),
    )(proj, cot)


def spread(value, target, row):
    count = value.shape[0]
    for lane in range(8):
        target[pl.ds(row * 8 + lane, count, stride=8), :] = value[:, lane * 128 : (lane + 1) * 128]


def spread_rows(source, target, row):
    def body(block, _):
        begin = pl.multiple_of(block * 16, 16)
        spread(source[pl.ds(begin, 16), :].astype(F32), target, row + begin)
        return 0

    lax.fori_loop(0, ROWS // 16, body, 0)


def gather_rows(source, target):
    def body(block, _):
        begin = pl.multiple_of(block * 16, 16)
        for lane in range(8):
            value = source[pl.ds(begin * 8 + lane, 16, stride=8), :]
            target[pl.ds(begin, 16), lane * 128 : (lane + 1) * 128] = value.astype(target.dtype)
        return 0

    lax.fori_loop(0, ROWS // 16, body, 0)


def tiles(ref, row, count):
    return ref[pl.ds(pl.multiple_of(row * 8, 8), count * 8), :].reshape(count, 8, 128)


def put_tiles(ref, row, value):
    ref[pl.ds(pl.multiple_of(row * 8, 8), value.shape[0] * 8), :] = value.reshape(-1, 128)


def total(value):
    parts = [value[n] for n in range(value.shape[0])]
    while len(parts) > 1:
        parts = [a + b for a, b in zip(parts[::2], parts[1::2])]
    return parts[0]


def edge_masks():
    me = lax.axis_index("ctx")
    return (me > 0).astype(F32), (me < lax.axis_size("ctx") - 1).astype(F32)


def first_kernel(proj, cot, prev, nextp, nextc, filt, decay, mixed, states, x, taps, c, g, gf):
    has_prev, has_next = edge_masks()
    for j in range(3):
        spread(prev[j].astype(F32) * has_prev, x.at[j], 0)
        spread_rows(proj.at[j], x.at[j], HALO)
        spread(nextp[j].astype(F32) * has_next, x.at[j], HALO + ROWS)
        spread(filt[j], taps.at[j], 0)
    spread_rows(cot, c, 0)
    spread(nextc[...].astype(F32) * has_next, c, ROWS)

    def conv(block, _):
        t = block * 8
        out = []
        for j in range(3):
            window = tiles(x.at[j], t + 2, 14)
            weight = tiles(taps.at[j], 0, TAPS)
            out.append(sum(weight[i][None] * window[6 - i : 14 - i] for i in range(TAPS)))
            put_tiles(mixed.at[j], t, out[j])
        put_tiles(g, t, out[1] * out[2])
        put_tiles(gf, t, tiles(c, t, 8) * out[0])
        return 0

    lax.fori_loop(0, EXT // 8, conv, 0)
    a = decay[0]

    def step(block, carry):
        s, b = carry
        ahead = tiles(g, block * 8, 8)
        behind = tiles(gf, EXT - 8 - block * 8, 8)
        for u in range(8):
            s = a * s + ahead[u][None]
            b = a * b + behind[7 - u][None]
        return s, b

    zero = jnp.zeros((POLES, 8, 128), F32)
    s, b = lax.fori_loop(0, ROWS // 8, step, (zero, zero))
    states[0] = s
    states[1] = b


def tile_spec(lead, width):
    return pl.BlockSpec(lead + (width,), lambda i: (0,) * len(lead) + (i,))


def first(proj, cot, prev, nextp, nextc, filt, tables):
    whole = pl.BlockSpec((4, POLES, 8, 128), lambda i: (0, 0, 0, 0))
    return pl.pallas_call(
        first_kernel,
        name="first",
        grid=(TILES,),
        out_shape=(
            jax.ShapeDtypeStruct((TILES, 3, EXT * 8, 128), F32),
            jax.ShapeDtypeStruct((2, POLES, TILES * 8, 128), F32),
        ),
        in_specs=[
            tile_spec((3, ROWS), 1024),
            tile_spec((ROWS,), 1024),
            tile_spec((3, HALO), 1024),
            tile_spec((3, HALO), 1024),
            tile_spec((HALO,), 1024),
            tile_spec((3, TAPS), 1024),
            whole,
        ],
        out_specs=(
            pl.BlockSpec((None, 3, EXT * 8, 128), lambda i: (i, 0, 0, 0)),
            pl.BlockSpec((2, POLES, 8, 128), lambda i: (0, 0, i, 0)),
        ),
        scratch_shapes=[
            pltpu.VMEM((3, (EXT + HALO) * 8, 128), F32),
            pltpu.VMEM((3, TAPS * 8, 128), F32),
            pltpu.VMEM((EXT * 8, 128), F32),
            pltpu.VMEM((EXT * 8, 128), F32),
            pltpu.VMEM((EXT * 8, 128), F32),
        ],
        compiler_params=pltpu.CompilerParams(vmem_limit_bytes=48 << 20),
    )(proj, cot, prev, nextp, nextc, filt, tables)


def place():
    dp, me = lax.axis_index("dp"), lax.axis_index("ctx")
    return dp, lax.div(me, 2), lax.rem(me, 2)


def remote(source, target, send_sem, recv_sem, dp, chip, core):
    return pltpu.make_async_remote_copy(
        src_ref=source,
        dst_ref=target,
        send_sem=send_sem,
        recv_sem=recv_sem,
        device_id=(dp, chip * 2 + core),
        device_id_type=MESH,
    )


def greet(dp, chip, core, lines):
    barrier = pltpu.get_barrier_semaphore()

    def plane(offset, _):
        other = lax.rem(chip + offset, CHIPS)
        pl.semaphore_signal(barrier, inc=1, device_id=(dp, other * 2 + core), device_id_type=MESH)
        return 0

    lax.fori_loop(1, CHIPS, plane, 0)
    pl.semaphore_signal(barrier, inc=1, device_id=(dp, chip * 2 + 1 - core), device_id_type=MESH)
    for offset in range(1, lines):
        other = lax.rem(dp + offset, lines)
        pl.semaphore_signal(barrier, inc=1, device_id=(other, chip * 2 + core), device_id_type=MESH)
    pl.semaphore_wait(barrier, CHIPS + lines - 1)


def exchange(source, target, send_sem, recv_sem, dp, chip, core, spread_source=True):
    def copy(other, slot):
        return remote(
            source.at[other] if spread_source else source,
            target.at[slot],
            send_sem.at[other],
            recv_sem.at[slot],
            dp,
            other,
            core,
        )

    def start(offset, _):
        copy(lax.rem(chip + offset, CHIPS), chip).start()
        return 0

    lax.fori_loop(1, CHIPS, start, 0)
    target[chip] = source[chip] if spread_source else source[...]

    def wait(offset, _):
        other = lax.rem(chip + CHIPS - offset, CHIPS)
        copy(other, other).wait_recv()
        return 0

    lax.fori_loop(1, CHIPS, wait, 0)

    def sent(offset, _):
        copy(lax.rem(chip + offset, CHIPS), chip).wait_send()
        return 0

    lax.fori_loop(1, CHIPS, sent, 0)


def scan_kernel(local, tables, out, partner, ends, came, back, entering, give, land, pair_send, pair_recv, send1, recv1, send2, recv2):
    dp, chip, core = place()
    half = TILES * 4
    mine, theirs = pl.ds(core * half, half), pl.ds((1 - core) * half, half)
    greet(dp, chip, core, 1)
    copy = remote(local.at[:, :, theirs, :], partner, pair_send.at[0], pair_recv.at[0], dp, chip, 1 - core)
    copy.start()
    copy.wait()
    low = core == 0

    def merge(n, _):
        d = tables[2, n][None]
        own = local[:, n, mine, :].reshape(2, TILES // 2, 8, 128)
        other = partner[:, n].reshape(2, TILES // 2, 8, 128)
        lo, hi = jnp.where(low, own, other), jnp.where(low, other, own)
        ends[n, 0] = (d * lo[0] + hi[0]).reshape(half, 128)
        ends[n, 1] = (lo[1] + d * hi[1]).reshape(half, 128)
        return 0

    lax.fori_loop(0, POLES, merge, 0)
    exchange(ends, came, send1, recv1, dp, chip, core)
    d2 = tables[3, chip][None]

    def ahead(q, s):
        back[q, 0] = s.reshape(half, 128)
        return d2 * s + came[q, 0].reshape(TILES // 2, 8, 128)

    def behind(k, s):
        q = CHIPS - 1 - k
        back[q, 1] = s.reshape(half, 128)
        return d2 * s + came[q, 1].reshape(TILES // 2, 8, 128)

    zero = jnp.zeros((TILES // 2, 8, 128), F32)
    lax.fori_loop(0, CHIPS, ahead, zero)
    lax.fori_loop(0, CHIPS, behind, zero)
    exchange(back, entering, send2, recv2, dp, chip, core)

    def split(n, _):
        d = tables[2, n][None]
        own = local[:, n, mine, :].reshape(2, TILES // 2, 8, 128)
        other = partner[:, n].reshape(2, TILES // 2, 8, 128)
        lo, hi = jnp.where(low, own, other), jnp.where(low, other, own)
        e = entering[n].reshape(2, TILES // 2, 8, 128)
        fwd_lo, fwd_hi = e[0], d * e[0] + lo[0]
        bwd_lo, bwd_hi = d * e[1] + hi[1], e[1]
        out[0, n, mine, :] = jnp.where(low, fwd_lo, fwd_hi).reshape(half, 128)
        out[1, n, mine, :] = jnp.where(low, bwd_lo, bwd_hi).reshape(half, 128)
        give[0, n] = jnp.where(low, fwd_hi, fwd_lo).reshape(half, 128)
        give[1, n] = jnp.where(low, bwd_hi, bwd_lo).reshape(half, 128)
        return 0

    lax.fori_loop(0, POLES, split, 0)
    copy = remote(give, land, pair_send.at[1], pair_recv.at[1], dp, chip, 1 - core)
    copy.start()
    copy.wait()
    out[:, :, theirs, :] = land[...]


def scan_states(states, tables):
    half = TILES * 4
    vmem = pl.BlockSpec(memory_space=pltpu.VMEM)
    pair = pltpu.VMEM((2, POLES, half, 128), F32)
    slots = pltpu.VMEM((CHIPS, 2, half, 128), F32)
    many = pltpu.SemaphoreType.DMA((CHIPS,))
    return pl.pallas_call(
        scan_kernel,
        name="scan_states",
        out_shape=jax.ShapeDtypeStruct(states.shape, F32),
        in_specs=[vmem, vmem],
        out_specs=vmem,
        scratch_shapes=[pair, slots, slots, slots, slots, pair, pair]
        + [pltpu.SemaphoreType.DMA((2,)), pltpu.SemaphoreType.DMA((2,)), many, many, many, many],
        compiler_params=pltpu.CompilerParams(
            collective_id=1, has_side_effects=True, vmem_limit_bytes=32 << 20
        ),
    )(states, tables)


def second_kernel(proj, cot, prev, nextc, filt, skip, tables, mixed, states, output, grad_proj, grads, x, taps, c, gm, o):
    has_prev, has_next = edge_masks()
    for j in range(3):
        spread(prev[j].astype(F32) * has_prev, x.at[j], 0)
        spread_rows(proj.at[j], x.at[j], HALO)
        spread(filt[j], taps.at[j], 0)
    spread_rows(cot, c, 0)
    spread(nextc[...].astype(F32) * has_next, c, ROWS)
    gain = skip[...]

    def step(block, carry):
        s, b = carry
        begin, end = block * 4, EXT - 4 - block * 4
        a, r = tables[0], tables[1]
        k0, v0 = tiles(mixed.at[1], begin, 4), tiles(mixed.at[2], begin, 4)
        g = k0 * v0
        gf = tiles(c, end, 4) * tiles(mixed.at[0], end, 4)
        fwd, bwd = [], []
        for u in range(4):
            s = a * s + g[u][None]
            b = a * b + gf[3 - u][None]
            fwd.append(total(r * s))
            bwd.append(total(r * b))
        filtered = jnp.stack(fwd) + gain[None] * g
        grad_gated = jnp.stack(bwd[::-1]) + gain[None] * gf
        put_tiles(o, begin, tiles(mixed.at[0], begin, 4) * filtered)
        put_tiles(gm.at[0], begin, tiles(c, begin, 4) * filtered)
        put_tiles(gm.at[1], end, grad_gated * tiles(mixed.at[2], end, 4))
        put_tiles(gm.at[2], end, grad_gated * tiles(mixed.at[1], end, 4))
        return s, b

    lax.fori_loop(0, EXT // 4, step, (states[0], states[1]))
    gather_rows(o, output)

    def skip_sum(block, acc):
        t = block * 8
        terms = tiles(c, t, 8) * tiles(mixed.at[0], t, 8) * (tiles(mixed.at[1], t, 8) * tiles(mixed.at[2], t, 8))
        return acc + total(terms)

    grads[pl.ds(21 * 8, 8), :] = lax.fori_loop(0, ROWS // 8, skip_sum, jnp.zeros((8, 128), F32))
    grads[pl.ds(22 * 8, 16), :] = jnp.zeros((16, 128), F32)
    for j in range(3):
        weight = tiles(taps.at[j], 0, TAPS)

        def conv(block, acc):
            t = block * 8
            ahead = tiles(gm.at[j], t, 14)
            window = tiles(x.at[j], t + 2, 14)
            put_tiles(o, t, sum(weight[i][None] * ahead[i : i + 8] for i in range(TAPS)))
            return tuple(acc[i] + total(ahead[:8] * window[6 - i : 14 - i]) for i in range(TAPS))

        acc = lax.fori_loop(0, ROWS // 8, conv, (jnp.zeros((8, 128), F32),) * TAPS)
        for i in range(TAPS):
            grads[pl.ds((j * TAPS + i) * 8, 8), :] = acc[i]
        gather_rows(o, grad_proj.at[j])


def second(proj, cot, prev, nextc, filt, skip, tables, mixed, states):
    return pl.pallas_call(
        second_kernel,
        name="second",
        grid=(TILES,),
        out_shape=(
            jax.ShapeDtypeStruct((ROWS, TILES * 1024), jnp.bfloat16),
            jax.ShapeDtypeStruct((3, ROWS, TILES * 1024), jnp.bfloat16),
            jax.ShapeDtypeStruct((TILES, GRADS * 8, 128), F32),
        ),
        in_specs=[
            tile_spec((3, ROWS), 1024),
            tile_spec((ROWS,), 1024),
            tile_spec((3, HALO), 1024),
            tile_spec((HALO,), 1024),
            tile_spec((3, TAPS), 1024),
            pl.BlockSpec((None, 8, 128), lambda i: (i, 0, 0)),
            pl.BlockSpec((4, POLES, 8, 128), lambda i: (0, 0, 0, 0)),
            pl.BlockSpec((None, 3, EXT * 8, 128), lambda i: (i, 0, 0, 0)),
            pl.BlockSpec((2, POLES, 8, 128), lambda i: (0, 0, i, 0)),
        ],
        out_specs=(
            tile_spec((ROWS,), 1024),
            tile_spec((3, ROWS), 1024),
            pl.BlockSpec((None, GRADS * 8, 128), lambda i: (i, 0, 0)),
        ),
        scratch_shapes=[
            pltpu.VMEM((3, (EXT + HALO) * 8, 128), F32),
            pltpu.VMEM((3, TAPS * 8, 128), F32),
            pltpu.VMEM((EXT * 8, 128), F32),
            pltpu.VMEM((3, EXT * 8, 128), F32),
            pltpu.VMEM((EXT * 8, 128), F32),
        ],
        compiler_params=pltpu.CompilerParams(vmem_limit_bytes=48 << 20),
    )(proj, cot, prev, nextc, filt, skip, tables, mixed, states)


def sum_kernel(grads, out, partner, slices, came, part, lines, around, land, pair_send, pair_recv, send1, recv1, line_send, line_recv, send2, recv2):
    dp, chip, core = place()
    depth = lax.axis_size("dp")
    half = TILES // 2
    mine, theirs = pl.ds(core * half, half), pl.ds((1 - core) * half, half)
    greet(dp, chip, core, depth)
    copy = remote(grads.at[theirs], partner, pair_send.at[0], pair_recv.at[0], dp, chip, 1 - core)
    copy.start()
    copy.wait()
    whole = grads[mine] + partner[...]
    slices[...] = whole.reshape(slices.shape)
    exchange(slices, came, send1, recv1, dp, chip, core)
    acc = came[0]
    for q in range(1, CHIPS):
        acc = acc + came[q]
    part[...] = acc

    def line(other, slot):
        return pltpu.make_async_remote_copy(
            src_ref=part,
            dst_ref=lines.at[slot],
            send_sem=line_send.at[other],
            recv_sem=line_recv.at[slot],
            device_id=(other, chip * 2 + core),
            device_id_type=MESH,
        )

    for offset in range(1, depth):
        line(lax.rem(dp + offset, depth), dp).start()
    lines[dp] = acc
    for offset in range(1, depth):
        other = lax.rem(dp + depth - offset, depth)
        line(other, other).wait_recv()
    for offset in range(1, depth):
        line(lax.rem(dp + offset, depth), dp).wait_send()
    acc = lines[0]
    for q in range(1, depth):
        acc = acc + lines[q]
    part[...] = acc
    exchange(part, around, send2, recv2, dp, chip, core, spread_source=False)
    copy = remote(around, land, pair_send.at[1], pair_recv.at[1], dp, chip, 1 - core)
    copy.start()
    out[mine] = around[...].reshape(whole.shape)
    copy.wait()
    out[theirs] = land[...].reshape(whole.shape)


def sum_grads(grads):
    vmem = pl.BlockSpec(memory_space=pltpu.VMEM)
    piece = TILES // 2 * GRADS * 8 // CHIPS
    slots = pltpu.VMEM((CHIPS, piece, 128), F32)
    many = pltpu.SemaphoreType.DMA((CHIPS,))
    few = pltpu.SemaphoreType.DMA((4,))
    two = pltpu.SemaphoreType.DMA((2,))
    return pl.pallas_call(
        sum_kernel,
        name="sum_grads",
        out_shape=jax.ShapeDtypeStruct(grads.shape, F32),
        in_specs=[vmem],
        out_specs=vmem,
        scratch_shapes=[
            pltpu.VMEM((TILES // 2, GRADS * 8, 128), F32),
            slots,
            slots,
            pltpu.VMEM((piece, 128), F32),
            pltpu.VMEM((4, piece, 128), F32),
            slots,
            slots,
            two,
            two,
            many,
            many,
            few,
            few,
            many,
            many,
        ],
        compiler_params=pltpu.CompilerParams(
            collective_id=2, has_side_effects=True, vmem_limit_bytes=32 << 20
        ),
    )(grads)


def coefficient_tables(residues, decay_rates):
    rates, weights = decay_rates.T, residues.T
    table = jnp.stack(
        [jnp.exp(-rates), weights, jnp.exp(-rates * ROWS), jnp.exp(-rates * (2 * ROWS))]
    ).reshape(4, POLES, 4, 128)
    return jnp.concatenate([table, table], axis=2)


def local(projected, short_filter, residues, decay_rates, skip_gain, cotangent):
    proj = jnp.transpose(projected[0], (1, 0, 2))
    cot = cotangent[0]
    channels = proj.shape[2]
    tables = coefficient_tables(residues, decay_rates)
    prev, nextp, nextc = halo(proj, cot)
    mixed, states = first(proj, cot, prev, nextp, nextc, short_filter, tables)
    states = scan_states(states, tables)
    skip = skip_gain.reshape(TILES, 8, 128)
    output, grad_proj, grads = second(proj, cot, prev, nextc, short_filter, skip, tables, mixed, states)
    sums = sum_grads(grads).reshape(TILES, GRADS, 1024).transpose(1, 0, 2).reshape(GRADS, channels)
    return (
        output[None],
        jnp.transpose(grad_proj, (1, 0, 2))[None],
        sums[:21].reshape(3, TAPS, channels),
        sums[21],
    )


def solution(mesh):
    placed = (P("dp", "ctx", None, None), P(), P(), P(), P(), P("dp", "ctx", None))
    return jax.shard_map(
        local,
        mesh=mesh,
        in_specs=placed,
        out_specs=(P("dp", "ctx", None), P("dp", "ctx", None, None), P(), P()),
        check_vma=False,
    )
```

time: 1430 us -> 151 us (0.11)
  waiting for transfers between devices: 604 us -> 0 us
  starting transfers between devices: 227 us -> 0 us
  other arithmetic: 199 us -> 0.83 us
  local copies, waits for them, and re-layouts: 160 us -> 6.27 us
  Pallas kernels: 0 us -> 143 us
  matrix products: 114 us -> 0 us
  blocking collectives: 102 us -> 0 us
    ppermute x64 -> x0, waiting for transfers between devices: 523 us -> none  [passed_along(): lax.ppermute(value, axis, [(source, source + steps) for source in range(f...]
    ppermute x64 -> x0, starting transfers between devices: 227 us -> none  [passed_along(): lax.ppermute(value, axis, [(source, source + steps) for source in range(f...]
    pallas_call x0 -> x5, Pallas kernels: none -> 143 us  [the longest x1 51.9 us: second(): pl.pallas_call(second_kernel, name='second', grid=(TILES,), out_shape=(ja...]
    dot_general x8 -> x0, matrix products: 114 us -> none  [the longest x1 29.5 us: forward_local(): jnp.einsum('gts,bkswg->bktwg', toeplitz, inputs, precision=HIGHEST)]
    psum x1 -> x0, blocking collectives: 102 us -> none  [local(): grad_short, grad_skip = lax.psum((short_local, skip_local), ('dp', 'ctx'))]
    psum x1 -> x0, waiting for transfers between devices: 80.9 us -> none  [local(): grad_short, grad_skip = lax.psum((short_local, skip_local), ('dp', 'ctx'))]
    unnamed x9 -> x0, other arithmetic: 43.6 us -> none
    reduce_sum x2 -> x0, other arithmetic: 41.5 us -> none  [the longest x1 27.9 us: filter_grad(): return jnp.sum(products, axis=(0, 1))]
  transfers between devices with their start and end apart: 65 -> 0, of which waited for: 63 -> 0; matrix products, arithmetic and copies ran while one was open for 9% -> 0% of each run, Pallas kernels for 0% -> 0%
where the time goes in v1:
time: 151 us
  Pallas kernels  143 us (95%)
  local copies, waits for them, and re-layouts  6.27 us (4%)
    pallas_call x1, Pallas kernels, second(): pl.pallas_call(second_kernel, name='second', grid=(TILES,), out_shape=(ja...  51.9 us
    pallas_call x1, Pallas kernels, scan_states(): pl.pallas_call(scan_kernel, name='scan_states', out_shape=jax.ShapeDtypeS...  30.5 us
    pallas_call x1, Pallas kernels, sum_grads(): pl.pallas_call(sum_kernel, name='sum_grads', out_shape=jax.ShapeDtypeStru...  26.5 us
    pallas_call x1, Pallas kernels, first(): pl.pallas_call(first_kernel, name='first', grid=(TILES,), out_shape=(jax....  24.1 us
    pallas_call x1, Pallas kernels, halo(): pl.pallas_call(halo_kernel, name='halo', out_shape=(jax.ShapeDtypeStruct(...  10.2 us

profile of v1, /device:TPU:1, one launch (start us, length us, event | category | flops | bytes accessed | tf_op | source)
XLA Modules:
  0.0 151.0 jit_solution(18150931139231654191)
XLA Ops:
  0.6 0.0 copy-start.1
  0.6 0.0 copy-start
  0.7 0.9 stack.16
  1.6 0.8 exponential_bitcast_fusion.2
  2.5 10.2 %halo.1 = (bf16[3,8,8192]{2,1,0:T(8,128)(2,1)}, bf16[3,8,8192]{2,1,0:T(8,128)(2,1)}, bf16[8,8192]{1,0:T(8,128)(2,1)}) custom-call(bf16[3,128,8192]{2,1,0:T(8,128)(2,1)} %bitcast.23, bf16[128,8192]{1,0:T(8,128)(2,1)} %bitcast.19), custom_call_target="tpu_custom_call" | custom-call | tf_op jit(solution)/shard_map/halo/pallas_call | solution.py:55
  12.7 0.0 copy-done.1
  12.7 0.0 copy-done
  12.7 0.0 copy-start.2
  12.8 1.0 copy-done.2
  13.7 0.0 copy-start.3
  13.7 0.9 copy-done.3
  14.7 0.0 copy-start.4
  14.7 1.0 copy-done.4
  15.6 0.0 copy-start.5
  15.6 24.1 %first.1 = (f32[8,3,1088,128]{3,2,1,0:T(8,128)}, f32[2,16,64,128]{3,2,1,0:T(8,128)S(1)}) custom-call(bf16[3,128,8192]{2,1,0:T(8,128)(2,1)} %bitcast.24, bf16[128,8192]{1,0:T(8,128)(2,1)S(1)} %bitcast.20, bf16[3,8,8192]{2,1,0:T(8,128)(2,1)S(1)} %copy-done.2, bf16[3,8,8192]{2,1,0:T(8,128)(2,1)S(1)} %copy-done.4, bf16[8,8192]{1,0:T(8,128)(2,1)S(1)} %copy-done.3, ...), custom_call_target="tpu_custom_call" | custom-call | tf_op jit(solution)/shard_map/first/pallas_call | solution.py:162
  39.7 30.5 %scan_states.1.states = f32[2,16,64,128]{3,2,1,0:T(8,128)S(1)} custom-call(f32[2,16,64,128]{3,2,1,0:T(8,128)S(1)} %get-tuple-element.16.local, f32[4,16,8,128]{3,2,1,0:T(8,128)S(1)} %maximum_maximum_fusion.decay.tables), custom_call_target="tpu_custom_call" | custom-call | tf_op jit(solution)/shard_map/scan_states/pallas_call | solution.py:323
  70.2 0.0 copy-done.5
  70.2 51.9 %second.1 = (bf16[128,8192]{1,0:T(8,128)(2,1)}, bf16[3,128,8192]{2,1,0:T(8,128)(2,1)}, f32[8,192,128]{2,1,0:T(8,128)S(1)}) custom-call(bf16[3,128,8192]{2,1,0:T(8,128)(2,1)} %bitcast.25, bf16[128,8192]{1,0:T(8,128)(2,1)S(1)} %bitcast.21, bf16[3,8,8192]{2,1,0:T(8,128)(2,1)S(1)} %copy-done.2, bf16[8,8192]{1,0:T(8,128)(2,1)S(1)} %copy-done.3, ...), custom_call_target="tpu_custom_call" | custom-call | tf_op jit(solution)/shard_map/second/pallas_call | solution.py:395
  122.1 26.5 %sum_grads.1 = f32[8,192,128]{2,1,0:T(8,128)S(1)} custom-call(f32[8,192,128]{2,1,0:T(8,128)S(1)} %get-tuple-element.19.grads), custom_call_target="tpu_custom_call" | custom-call | tf_op jit(solution)/shard_map/sum_grads/pallas_call | solution.py:485
  148.6 0.1 reshape.32
  148.7 0.6 slice.11
  149.4 0.4 copy.10
  149.8 1.2 reshape.33
  (4 shorter events, 0.1 us)
Async XLA Ops:
  0.6 12.1 %copy-start.1 = (f32[3,7,8192]{2,1,0:T(8,128)S(1)}, f32[3,7,8192]{2,1,0:T(8,128)}, u32[]{:S(2)}) copy-start(f32[3,7,8192]{2,1,0:T(8,128)} %filt.3) | copy-start | bytes 2064388
  0.6 12.1 %copy-start = (bf16[1,128,8192]{2,1,0:T(8,128)(2,1)S(1)}, bf16[1,128,8192]{2,1,0:T(8,128)(2,1)}, u32[]{:S(2)}) copy-start(bf16[1,128,8192]{2,1,0:T(8,128)(2,1)} %param.11) | copy-start | bytes 6291460
  12.7 1.0 copy-start.2
  13.7 0.9 copy-start.3
  14.7 1.0 copy-start.4
  15.6 54.6 %copy-start.5 = (f32[8192]{0:T(1024)S(1)}, f32[8192]{0:T(1024)}, u32[]{:S(2)}) copy-start(f32[8192]{0:T(1024)} %param.10) | copy-start | bytes 98308

commit v2 on v0

v2 whole, which is shorter than its diff:
```python
import jax
import jax.numpy as jnp
from jax import lax
from jax.experimental import pallas as pl
from jax.experimental.pallas import tpu as pltpu
from jax.sharding import PartitionSpec as P

MESH = pl.DeviceIdType.MESH
F32 = jnp.float32
BF16 = jnp.bfloat16
ROWS = 128
HALO = 8
EXT = ROWS + HALO
TILES = 8
WIDE = 1024
POLES = 16
TAPS = 7
CHIPS = 16
LINES = 4
GRADS = 24
GROUPS = 4
SUMS = 2
PIECE = TILES // SUMS // 2 * GRADS * 8 // CHIPS


def spread(value, target, row):
    count = value.shape[0]
    for lane in range(8):
        target[pl.ds(row * 8 + lane, count, stride=8), :] = value[:, lane * 128 : (lane + 1) * 128]


def spread_rows(source, target, row):
    def body(block, _):
        begin = pl.multiple_of(block * 16, 16)
        spread(source[pl.ds(begin, 16), :].astype(F32), target, row + begin)
        return 0

    lax.fori_loop(0, ROWS // 16, body, 0)


def gather_rows(source, target):
    def body(block, _):
        begin = pl.multiple_of(block * 16, 16)
        for lane in range(8):
            value = source[pl.ds(begin * 8 + lane, 16, stride=8), :]
            target[pl.ds(begin, 16), lane * 128 : (lane + 1) * 128] = value.astype(target.dtype)
        return 0

    lax.fori_loop(0, ROWS // 16, body, 0)


def tiles(ref, row, count):
    return ref[pl.ds(pl.multiple_of(row * 8, 8), count * 8), :].reshape(count, 8, 128)


def put_tiles(ref, row, value):
    ref[pl.ds(pl.multiple_of(row * 8, 8), value.shape[0] * 8), :] = value.reshape(-1, 128)


def total(value):
    while value.shape[0] > 1:
        half = value.shape[0] // 2
        value = value[:half] + value[half:]
    return value[0]


def kernel(
    proj, cot, filt, skip, rates, weights,
    output, grad_proj, grad_short, grad_skip,
    x, mix, c, yf, yb, ins, outs, prev, nextp, nextc, taps, tables,
    st, st_pair, st_ends, st_came, st_back, st_enter, st_give, st_land, ea,
    gr, gr_pair, gr_cut, gr_came, gr_part, gr_whole, gr_lines, gr_around, gr_land,
    in_sem, out_sem, halo_send, halo_recv,
    st_ps, st_pr, st_s1, st_r1, st_s2, st_r2, st_ls, st_lr,
    gr_ps, gr_pr, gr_s1, gr_r1, gr_s2, gr_r2, gr_ls, gr_lr,
):
    dp, me = lax.axis_index("dp"), lax.axis_index("ctx")
    count = 2 * CHIPS
    chip, core = lax.div(me, 2), lax.rem(me, 2)
    low = core == 0
    up, down = lax.rem(me + 1, count), lax.rem(me + count - 1, count)
    has_prev = (me > 0).astype(F32)
    has_next = (me < count - 1).astype(F32)

    def remote(source, target, send_sem, recv_sem, line, ctx):
        return pltpu.make_async_remote_copy(
            src_ref=source,
            dst_ref=target,
            send_sem=send_sem,
            recv_sem=recv_sem,
            device_id=(line, ctx),
            device_id_type=MESH,
        )

    barrier = pltpu.get_barrier_semaphore()

    def greet(offset, _):
        other = lax.rem(chip + offset, CHIPS) * 2 + core
        pl.semaphore_signal(barrier, inc=1, device_id=(dp, other), device_id_type=MESH)
        return 0

    lax.fori_loop(1, CHIPS, greet, 0)
    for other in (chip * 2 + 1 - core, up, down):
        pl.semaphore_signal(barrier, inc=1, device_id=(dp, other), device_id_type=MESH)
    for offset in range(1, LINES):
        line = lax.rem(dp + offset, LINES)
        pl.semaphore_signal(barrier, inc=1, device_id=(line, me), device_id_type=MESH)

    def fetch(tile):
        slot = lax.rem(tile, 2)
        lanes = pl.ds(pl.multiple_of(tile * WIDE, WIDE), WIDE)
        return (
            pltpu.make_async_copy(proj.at[:, :, lanes], ins.at[slot, pl.ds(0, 3)], in_sem.at[slot, 0]),
            pltpu.make_async_copy(cot.at[:, lanes], ins.at[slot, 3], in_sem.at[slot, 1]),
        )

    for tile in range(2):
        for copy in fetch(tile):
            copy.start()

    for quarter in range(4):
        lanes = slice(quarter * 128, (quarter + 1) * 128)
        rate = rates[:, lanes]
        rows = (jnp.exp(-rate), weights[:, lanes], jnp.exp(-rate * ROWS), jnp.exp(-rate * (2 * ROWS)))
        for k in range(4):
            for again in (0, 4):
                tables[k, pl.ds(quarter + again, POLES, stride=8), :] = rows[k]

    def table(k):
        return tables[k].reshape(POLES, 8, 128)

    def short_filter(tile, block):
        t = block * 8
        for j in range(3):
            window = tiles(x.at[tile, j], t + 2, 14)
            weight = tiles(taps.at[tile, j], 0, TAPS)
            part = weight[0][None] * window[6:14]
            for i in range(1, TAPS):
                part = part + weight[i][None] * window[6 - i : 14 - i]
            put_tiles(mix.at[tile, j], t, part)

    def load_tile(tile):
        slot = lax.rem(tile, 2)
        for copy in fetch(tile):
            copy.wait()
        lanes = pl.ds(pl.multiple_of(tile * WIDE, WIDE), WIDE)
        for j in range(3):
            spread_rows(ins.at[slot, j], x.at[tile, j], HALO)
            spread(filt[j, :, lanes], taps.at[tile, j], 0)
        spread_rows(ins.at[slot, 3], c.at[tile], 0)

        @pl.when(tile < TILES - 2)
        def _():
            for copy in fetch(tile + 2):
                copy.start()

        def inner(block, _):
            short_filter(tile, block)
            return 0

        lax.fori_loop(1, ROWS // 8, inner, 0)

    pl.semaphore_wait(barrier, CHIPS - 1 + 3 + LINES - 1)
    last, first = pl.ds(ROWS - HALO, HALO), pl.ds(0, HALO)
    halo = (
        remote(proj.at[:, last, :], prev, halo_send.at[0], halo_recv.at[0], dp, up),
        remote(proj.at[:, first, :], nextp, halo_send.at[1], halo_recv.at[1], dp, down),
        remote(cot.at[first, :], nextc, halo_send.at[2], halo_recv.at[2], dp, down),
    )
    for copy in halo:
        copy.start()

    def load_loop(tile, _):
        load_tile(tile)
        return 0

    lax.fori_loop(0, TILES, load_loop, 0)
    for copy in halo:
        copy.wait()

    def plane_send(source, target, send_sem, recv_sem):
        def start(offset, _):
            other = lax.rem(chip + offset, CHIPS)
            remote(source(other), target.at[chip], send_sem, recv_sem, dp, other * 2 + core).start()
            return 0

        lax.fori_loop(1, CHIPS, start, 0)
        target[chip] = source(chip)[...]

    def plane_wait(target, send_sem, recv_sem):
        most = target.at[pl.ds(0, CHIPS - 1)]
        copy = remote(most, most, send_sem, recv_sem, dp, me)
        copy.wait_recv()
        copy.wait_send()

    pair = chip * 2 + 1 - core

    def mine(group):
        return pl.ds(pl.multiple_of((group * 2 + core) * 8, 8), 8)

    def theirs(group):
        return pl.ds(pl.multiple_of((group * 2 + 1 - core) * 8, 8), 8)

    def st_pair_copy(g):
        return remote(st.at[:, :, theirs(g), :], st_pair.at[g], st_ps.at[g], st_pr.at[g], dp, pair)

    def st_back_copy(g):
        return remote(st_give.at[g], st_land.at[g], st_ls.at[g], st_lr.at[g], dp, pair)

    def low_high(g):
        own, other = st[:, :, mine(g), :], st_pair[g]
        return jnp.where(low, own, other), jnp.where(low, other, own)

    def st_1(g):
        st_pair_copy(g).start()

    def st_2(g):
        st_pair_copy(g).wait()
        lo, hi = low_high(g)
        d = table(2)
        st_ends[g, :, 0] = d * lo[0] + hi[0]
        st_ends[g, :, 1] = lo[1] + d * hi[1]
        plane_send(lambda q: st_ends.at[g, q], st_came.at[g], st_s1.at[g], st_r1.at[g])

    def st_3(g):
        plane_wait(st_came.at[g], st_s1.at[g], st_r1.at[g])
        d2 = tables[3, pl.ds(pl.multiple_of(chip * 8, 8), 8), :]
        s = jnp.zeros((8, 128), F32)
        for q in range(CHIPS):
            st_back[g, q, 0] = s
            s = d2 * s + st_came[g, q, 0]
        s = jnp.zeros((8, 128), F32)
        for q in reversed(range(CHIPS)):
            st_back[g, q, 1] = s
            s = d2 * s + st_came[g, q, 1]
        plane_send(lambda q: st_back.at[g, q], st_enter.at[g], st_s2.at[g], st_r2.at[g])

    def st_4(g):
        plane_wait(st_enter.at[g], st_s2.at[g], st_r2.at[g])
        lo, hi = low_high(g)
        d = table(2)
        fwd, bwd = st_enter[g, :, 0], st_enter[g, :, 1]
        fwd_hi, bwd_lo = d * fwd + lo[0], d * bwd + hi[1]
        ea[0, :, mine(g), :] = jnp.where(low, fwd, fwd_hi)
        ea[1, :, mine(g), :] = jnp.where(low, bwd_lo, bwd)
        st_give[g, 0] = jnp.where(low, fwd_hi, fwd)
        st_give[g, 1] = jnp.where(low, bwd, bwd_lo)
        st_back_copy(g).start()

    def st_5(g):
        st_back_copy(g).wait()
        ea[:, :, theirs(g), :] = st_land[g]

    def st_hooks(slot):
        step = lax.div(slot, 2)
        even = lax.rem(slot, 2) == 0

        @pl.when(jnp.logical_and(even, jnp.logical_and(step >= 3, step < GROUPS + 3)))
        def _():
            st_4(step - 3)

        @pl.when(jnp.logical_and(even, jnp.logical_and(step >= 2, step < GROUPS + 2)))
        def _():
            st_3(step - 2)

        @pl.when(jnp.logical_and(even, jnp.logical_and(step >= 1, step < GROUPS + 1)))
        def _():
            st_2(step - 1)

    def local_scan(tile):
        q, k, v = mix.at[tile, 0], mix.at[tile, 1], mix.at[tile, 2]

        def step(block, carry):
            s, b = carry
            begin, end = block * 4, EXT - 4 - block * 4
            a, r = table(0), table(1)
            g = tiles(k, begin, 4) * tiles(v, begin, 4)
            gf = tiles(c.at[tile], end, 4) * tiles(q, end, 4)
            fwd, bwd = [], []
            for u in range(4):
                s = a * s + g[u][None]
                b = a * b + gf[3 - u][None]
                fwd.append(total(r * s))
                bwd.append(total(r * b))
            put_tiles(yf.at[tile], begin, jnp.stack(fwd))
            put_tiles(yb.at[tile], end, jnp.stack(bwd[::-1]))
            return s, b

        zero = jnp.zeros((POLES, 8, 128), F32)
        s, b = lax.fori_loop(0, ROWS // 4, step, (zero, zero))
        rows = pl.ds(pl.multiple_of(tile * 8, 8), 8)
        st[0, :, rows, :] = s
        st[1, :, rows, :] = b
        lax.fori_loop(ROWS // 4, EXT // 4, step, (s, b))

    def scan_loop(tile, _):
        lanes = pl.ds(pl.multiple_of(tile * WIDE, WIDE), WIDE)
        for j in range(3):
            spread(prev[j, :, lanes].astype(F32) * has_prev, x.at[tile, j], 0)
            spread(nextp[j, :, lanes].astype(F32) * has_next, x.at[tile, j], HALO + ROWS)
        spread(nextc[:, lanes].astype(F32) * has_next, c.at[tile], ROWS)

        def edge(block, _):
            short_filter(tile, block * (ROWS // 8))
            return 0

        lax.fori_loop(0, 2, edge, 0)
        local_scan(tile)

        @pl.when(lax.rem(tile, 2) == 1)
        def _():
            st_1(lax.div(tile, 2))

        st_hooks(tile)
        return 0

    lax.fori_loop(0, TILES, scan_loop, 0)

    half = TILES // SUMS // 2

    def own(h):
        return pl.ds(h * 2 * half + core * half, half)

    def others(h):
        return pl.ds(h * 2 * half + (1 - core) * half, half)

    def gr_pair_copy(h):
        return remote(gr.at[others(h)], gr_pair.at[h], gr_ps.at[h, 0], gr_pr.at[h, 0], dp, pair)

    def gr_back_copy(h):
        return remote(gr_around.at[h], gr_land.at[h], gr_ps.at[h, 1], gr_pr.at[h, 1], dp, pair)

    def gr_1(h):
        gr_pair_copy(h).start()

    def gr_2(h):
        gr_pair_copy(h).wait()
        gr_cut[h] = (gr[own(h)] + gr_pair[h]).reshape(CHIPS, PIECE, 128)
        plane_send(lambda q: gr_cut.at[h, q], gr_came.at[h], gr_s1.at[h], gr_r1.at[h])

    def line_copy(h, other, slot):
        return remote(gr_part.at[h], gr_lines.at[h, slot], gr_ls.at[h, other], gr_lr.at[h, slot], other, me)

    def gr_3(h):
        plane_wait(gr_came.at[h], gr_s1.at[h], gr_r1.at[h])
        part = gr_came[h, 0]
        for q in range(1, CHIPS):
            part = part + gr_came[h, q]
        gr_part[h] = part
        gr_lines[h, dp] = part
        for offset in range(1, LINES):
            line_copy(h, lax.rem(dp + offset, LINES), dp).start()

    def gr_4(h):
        for offset in range(1, LINES):
            other = lax.rem(dp + offset, LINES)
            line_copy(h, other, other).wait_recv()
            line_copy(h, other, dp).wait_send()
        part = gr_lines[h, 0]
        for q in range(1, LINES):
            part = part + gr_lines[h, q]
        gr_whole[h] = part
        plane_send(lambda q: gr_whole.at[h], gr_around.at[h], gr_s2.at[h], gr_r2.at[h])

    def gr_5(h):
        plane_wait(gr_around.at[h], gr_s2.at[h], gr_r2.at[h])
        gr_back_copy(h).start()

    def gr_6(h):
        gr_back_copy(h).wait()
        gr[own(h)] = gr_around[h].reshape(half, GRADS * 8, 128)
        gr[others(h)] = gr_land[h].reshape(half, GRADS * 8, 128)

    def correct(tile):
        q, k, v = mix.at[tile, 0], mix.at[tile, 1], mix.at[tile, 2]
        rows = pl.ds(pl.multiple_of(tile * 8, 8), 8)
        gain = skip[rows, :][None]

        def ahead(block, carry):
            e, acc = carry
            t = block * 4
            a = table(0)
            more = []
            for _ in range(4):
                e = a * e
                more.append(total(e))
            g = tiles(k, t, 4) * tiles(v, t, 4)
            query, upstream = tiles(q, t, 4), tiles(c.at[tile], t, 4)
            filtered = tiles(yf.at[tile], t, 4) + jnp.stack(more) + gain * g
            gf = upstream * query
            put_tiles(yf.at[tile], t, query * filtered)
            put_tiles(c.at[tile], t, upstream * filtered)
            put_tiles(q, t, gf)
            return e, acc + total(gf * g)

        start = table(1) * ea[0, :, rows, :]
        e, acc = lax.fori_loop(0, ROWS // 4, ahead, (start, jnp.zeros((8, 128), F32)))
        gr[tile, pl.ds(21 * 8, 8), :] = acc
        gr[tile, pl.ds(22 * 8, 16), :] = jnp.zeros((16, 128), F32)
        lax.fori_loop(ROWS // 4, EXT // 4, ahead, (e, acc))

        def behind(block, e):
            t = EXT - 4 - block * 4
            a = table(0)
            more = []
            for _ in range(4):
                e = a * e
                more.append(total(e))
            grad_gated = tiles(yb.at[tile], t, 4) + jnp.stack(more[::-1]) + gain * tiles(q, t, 4)
            key, value = tiles(k, t, 4), tiles(v, t, 4)
            put_tiles(k, t, grad_gated * value)
            put_tiles(v, t, grad_gated * key)
            return e

        lax.fori_loop(0, EXT // 4, behind, table(1) * ea[1, :, rows, :])

    def mixed_grad(tile, j):
        return c.at[tile] if j == 0 else mix.at[tile, j]

    def tap_grads(tile):
        for j in range(3):

            def body(block, acc):
                t = block * 8
                grad = tiles(mixed_grad(tile, j), t, 8)
                window = tiles(x.at[tile, j], t + 2, 14)
                return tuple(acc[i] + total(grad * window[6 - i : 14 - i]) for i in range(TAPS))

            acc = lax.fori_loop(0, ROWS // 8, body, (jnp.zeros((8, 128), F32),) * TAPS)
            for i in range(TAPS):
                gr[tile, pl.ds((j * TAPS + i) * 8, 8), :] = acc[i]

    def post_loop(tile, _):
        @pl.when(lax.rem(tile, 2) == 0)
        def _():
            st_5(lax.div(tile, 2))

        correct(tile)
        tap_grads(tile)
        st_hooks(tile + TILES)

        @pl.when(tile == 3)
        def _():
            gr_1(0)

        @pl.when(tile == 4)
        def _():
            gr_2(0)

        @pl.when(tile == 6)
        def _():
            gr_3(0)

        return 0

    lax.fori_loop(0, TILES, post_loop, 0)
    gr_1(1)

    def leave(tile):
        slot = lax.rem(tile, 2)
        lanes = pl.ds(pl.multiple_of(tile * WIDE, WIDE), WIDE)
        return (
            pltpu.make_async_copy(outs.at[slot, pl.ds(0, 3)], grad_proj.at[:, :, lanes], out_sem.at[slot, 0]),
            pltpu.make_async_copy(outs.at[slot, 3], output.at[:, lanes], out_sem.at[slot, 1]),
        )

    def out_loop(tile, _):
        slot = lax.rem(tile, 2)

        @pl.when(tile >= 2)
        def _():
            for copy in leave(tile - 2):
                copy.wait()

        for j in range(3):

            def body(block, _):
                t = block * 8
                ahead = tiles(mixed_grad(tile, j), t, 14)
                weight = tiles(taps.at[tile, j], 0, TAPS)
                part = weight[0][None] * ahead[0:8]
                for i in range(1, TAPS):
                    part = part + weight[i][None] * ahead[i : i + 8]
                put_tiles(x.at[tile, j], t, part)
                return 0

            lax.fori_loop(0, ROWS // 8, body, 0)
            gather_rows(x.at[tile, j], outs.at[slot, j])
        gather_rows(yf.at[tile], outs.at[slot, 3])
        for copy in leave(tile):
            copy.start()

        @pl.when(tile == 0)
        def _():
            gr_4(0)
            gr_2(1)

        @pl.when(tile == 4)
        def _():
            gr_5(0)
            gr_3(1)

        @pl.when(tile == 6)
        def _():
            gr_6(0)

        return 0

    lax.fori_loop(0, TILES, out_loop, 0)
    gr_4(1)
    gr_5(1)
    for tile in range(TILES - 2, TILES):
        for copy in leave(tile):
            copy.wait()
    gr_6(1)
    for tile in range(TILES):
        grad_skip[tile * 8 : tile * 8 + 8, :] = gr[tile, 21 * 8 : 22 * 8, :]
        for j in range(3):
            for lane in range(8):
                value = gr[tile, pl.ds(j * TAPS * 8 + lane, TAPS, stride=8), :]
                begin = tile * WIDE + lane * 128
                grad_short[j, :, begin : begin + 128] = value


def whole(proj, cot, filt, skip, rates, weights):
    channels = proj.shape[2]
    anywhere = pl.BlockSpec(memory_space=pl.ANY)
    vmem = pl.BlockSpec(memory_space=pltpu.VMEM)

    def buffer(*shape, kind=F32):
        return pltpu.VMEM(shape, kind)

    def dma(*shape):
        return pltpu.SemaphoreType.DMA(shape)

    return pl.pallas_call(
        kernel,
        name="hyena",
        out_shape=(
            jax.ShapeDtypeStruct((ROWS, channels), BF16),
            jax.ShapeDtypeStruct((3, ROWS, channels), BF16),
            jax.ShapeDtypeStruct((3, TAPS, channels), F32),
            jax.ShapeDtypeStruct((TILES * 8, 128), F32),
        ),
        in_specs=[anywhere, anywhere, vmem, vmem, vmem, vmem],
        out_specs=(anywhere, anywhere, vmem, vmem),
        scratch_shapes=[
            buffer(TILES, 3, (EXT + HALO) * 8, 128),
            buffer(TILES, 3, EXT * 8, 128),
            buffer(TILES, EXT * 8, 128),
            buffer(TILES, EXT * 8, 128),
            buffer(TILES, EXT * 8, 128),
            buffer(2, 4, ROWS, WIDE, kind=BF16),
            buffer(2, 4, ROWS, WIDE, kind=BF16),
            buffer(3, HALO, channels, kind=BF16),
            buffer(3, HALO, channels, kind=BF16),
            buffer(HALO, channels, kind=BF16),
            buffer(TILES, 3, TAPS * 8, 128),
            buffer(4, POLES * 8, 128),
            buffer(2, POLES, TILES * 8, 128),
            buffer(GROUPS, 2, POLES, 8, 128),
            buffer(GROUPS, CHIPS, 2, 8, 128),
            buffer(GROUPS, CHIPS, 2, 8, 128),
            buffer(GROUPS, CHIPS, 2, 8, 128),
            buffer(GROUPS, CHIPS, 2, 8, 128),
            buffer(GROUPS, 2, POLES, 8, 128),
            buffer(GROUPS, 2, POLES, 8, 128),
            buffer(2, POLES, TILES * 8, 128),
            buffer(TILES, GRADS * 8, 128),
            buffer(SUMS, TILES // SUMS // 2, GRADS * 8, 128),
            buffer(SUMS, CHIPS, PIECE, 128),
            buffer(SUMS, CHIPS, PIECE, 128),
            buffer(SUMS, PIECE, 128),
            buffer(SUMS, PIECE, 128),
            buffer(SUMS, LINES, PIECE, 128),
            buffer(SUMS, CHIPS, PIECE, 128),
            buffer(SUMS, CHIPS, PIECE, 128),
            dma(2, 2),
            dma(2, 2),
            dma(3),
            dma(3),
        ]
        + [dma(GROUPS)] * 8
        + [dma(SUMS, 2)] * 2
        + [dma(SUMS)] * 4
        + [dma(SUMS, LINES)] * 2,
        compiler_params=pltpu.CompilerParams(
            collective_id=0, has_side_effects=True, vmem_limit_bytes=60 << 20
        ),
    )(proj, cot, filt, skip, rates, weights)


def local(projected, short_filter, residues, decay_rates, skip_gain, cotangent):
    proj = jnp.transpose(projected[0], (1, 0, 2))
    skip = skip_gain.reshape(TILES * 8, 128)
    output, grad_proj, grad_short, grad_skip = whole(
        proj, cotangent[0], short_filter, skip, decay_rates.T, residues.T
    )
    return (
        output[None],
        jnp.transpose(grad_proj, (1, 0, 2))[None],
        grad_short,
        grad_skip.reshape(skip_gain.shape),
    )


def solution(mesh):
    placed = (P("dp", "ctx", None, None), P(), P(), P(), P(), P("dp", "ctx", None))
    return jax.shard_map(
        local,
        mesh=mesh,
        in_specs=placed,
        out_specs=(P("dp", "ctx", None), P("dp", "ctx", None, None), P(), P()),
        check_vma=False,
    )
```

time: 1430 us -> 102 us (0.07)
  waiting for transfers between devices: 604 us -> 0 us
  starting transfers between devices: 227 us -> 0 us
  other arithmetic: 199 us -> 0 us
  local copies, waits for them, and re-layouts: 160 us -> 10.9 us
  matrix products: 114 us -> 0 us
  blocking collectives: 102 us -> 0 us
  Pallas kernels: 0 us -> 90 us
    ppermute x64 -> x0, waiting for transfers between devices: 523 us -> none  [passed_along(): lax.ppermute(value, axis, [(source, source + steps) for source in range(f...]
    ppermute x64 -> x0, starting transfers between devices: 227 us -> none  [passed_along(): lax.ppermute(value, axis, [(source, source + steps) for source in range(f...]
    dot_general x8 -> x0, matrix products: 114 us -> none  [the longest x1 29.5 us: forward_local(): jnp.einsum('gts,bkswg->bktwg', toeplitz, inputs, precision=HIGHEST)]
    psum x1 -> x0, blocking collectives: 102 us -> none  [local(): grad_short, grad_skip = lax.psum((short_local, skip_local), ('dp', 'ctx'))]
    pallas_call x0 -> x1, Pallas kernels: none -> 90 us  [whole(): pl.pallas_call(kernel, name='hyena', out_shape=(jax.ShapeDtypeStruct((ROW...]
    psum x1 -> x0, waiting for transfers between devices: 80.9 us -> none  [local(): grad_short, grad_skip = lax.psum((short_local, skip_local), ('dp', 'ctx'))]
    unnamed x9 -> x0, other arithmetic: 43.6 us -> none
    reduce_sum x2 -> x0, other arithmetic: 41.5 us -> none  [the longest x1 27.9 us: filter_grad(): return jnp.sum(products, axis=(0, 1))]
  transfers between devices with their start and end apart: 65 -> 0, of which waited for: 63 -> 0; matrix products, arithmetic and copies ran while one was open for 9% -> 0% of each run, Pallas kernels for 0% -> 0%
where the time goes in v2:
time: 102 us; the launch traced here: 101 us
  Pallas kernels  90 us (88%)
  local copies, waits for them, and re-layouts  10.9 us (11%)
    pallas_call x1, Pallas kernels, whole(): pl.pallas_call(kernel, name='hyena', out_shape=(jax.ShapeDtypeStruct((ROW...  90 us
    unnamed x8, local copies, waits for them, and re-layouts  10.9 us

profile of v2, /device:TPU:1, one launch (start us, length us, event | category | flops | bytes accessed | tf_op | source)
XLA Modules:
  0.0 101.5 jit_solution(16844656494956944210)
XLA Ops:
  0.6 90.0 %hyena.1 = (bf16[128,8192]{1,0:T(8,128)(2,1)}, bf16[3,128,8192]{2,1,0:T(8,128)(2,1)}, f32[3,7,8192]{2,1,0:T(8,128)}, f32[64,128]{1,0:T(8,128)}) custom-call(bf16[3,128,8192]{2,1,0:T(8,128)(2,1)} %bitcast.12, bf16[128,8192]{1,0:T(8,128)(2,1)} %bitcast.15, f32[3,7,8192]{2,1,0:T(8,128)} %filt.1, f32[64,128]{1,0:T(8,128)} %bitcast.16, f32[16,512]{1,0:T(8,128)} %bitcast.17, ...), custom_call_target="tpu_custom_call" | custom-call | tf_op jit(solution)/shard_map/hyena/pallas_call | solution.py:536
  90.6 3.1 %copy.14 = bf16[1,128,8192]{2,1,0:T(8,128)(2,1)} copy(bf16[1,128,8192]{2,1,0:T(8,128)(2,1)} %bitcast.14) | data formatting | bytes 4194304
  93.7 0.0 copy-start
  93.7 0.0 copy-start.1
  93.7 6.3 %copy.15 = bf16[1,128,3,8192]{3,1,2,0:T(8,128)(2,1)} copy(bf16[1,128,3,8192]{3,1,2,0:T(8,128)(2,1)} %bitcast.13) | data formatting | bytes 12582912
  100.0 0.0 copy-done
  100.0 0.9 copy.16
  100.9 0.0 copy-done.1
  100.9 0.6 copy.17
Async XLA Ops:
  93.7 6.3 %copy-start = (f32[3,7,8192]{2,1,0:T(8,128)S(1)}, f32[3,7,8192]{2,1,0:T(8,128)}, u32[]{:S(2)}) copy-start(f32[3,7,8192]{2,1,0:T(8,128)} %get-tuple-element.18) | copy-start | bytes 2064388
  93.7 7.2 %copy-start.1 = (f32[64,128]{1,0:T(8,128)S(1)}, f32[64,128]{1,0:T(8,128)}, u32[]{:S(2)}) copy-start(f32[64,128]{1,0:T(8,128)} %get-tuple-element.11) | copy-start | bytes 98308

commit v3 on v2

--- a/solution.py
+++ b/solution.py
@@ -20,6 +20,7 @@
 GRADS = 24
 GROUPS = 4
 SUMS = 2
+EARLY = 2
 PIECE = TILES // SUMS // 2 * GRADS * 8 // CHIPS
 
 
@@ -27,26 +28,6 @@
     count = value.shape[0]
     for lane in range(8):
         target[pl.ds(row * 8 + lane, count, stride=8), :] = value[:, lane * 128 : (lane + 1) * 128]
-
-
-def spread_rows(source, target, row):
-    def body(block, _):
-        begin = pl.multiple_of(block * 16, 16)
-        spread(source[pl.ds(begin, 16), :].astype(F32), target, row + begin)
-        return 0
-
-    lax.fori_loop(0, ROWS // 16, body, 0)
-
-
-def gather_rows(source, target):
-    def body(block, _):
-        begin = pl.multiple_of(block * 16, 16)
-        for lane in range(8):
-            value = source[pl.ds(begin * 8 + lane, 16, stride=8), :]
-            target[pl.ds(begin, 16), lane * 128 : (lane + 1) * 128] = value.astype(target.dtype)
-        return 0
-
-    lax.fori_loop(0, ROWS // 16, body, 0)
 
 
 def tiles(ref, row, count):
@@ -66,11 +47,11 @@
 
 def kernel(
     proj, cot, filt, skip, rates, weights,
-    output, grad_proj, grad_short, grad_skip,
-    x, mix, c, yf, yb, ins, outs, prev, nextp, nextc, taps, tables,
-    st, st_pair, st_ends, st_came, st_back, st_enter, st_give, st_land, ea,
-    gr, gr_pair, gr_cut, gr_came, gr_part, gr_whole, gr_lines, gr_around, gr_land,
-    in_sem, out_sem, halo_send, halo_recv,
+    outs, gr,
+    x, mix, c, yf, yb, ins, fins, prev, nextp, nextc, taps, tables, powers,
+    st, st_pair, st_ends, st_came, st_back, st_enter, st_give, st_land,
+    gr_pair, gr_cut, gr_came, gr_part, gr_whole, gr_lines, gr_around, gr_land,
+    in_sem, halo_send, halo_recv,
     st_ps, st_pr, st_s1, st_r1, st_s2, st_r2, st_ls, st_lr,
     gr_ps, gr_pr, gr_s1, gr_r1, gr_s2, gr_r2, gr_ls, gr_lr,
 ):
@@ -112,6 +93,7 @@
         return (
             pltpu.make_async_copy(proj.at[:, :, lanes], ins.at[slot, pl.ds(0, 3)], in_sem.at[slot, 0]),
             pltpu.make_async_copy(cot.at[:, lanes], ins.at[slot, 3], in_sem.at[slot, 1]),
+            pltpu.make_async_copy(filt.at[:, :, lanes], fins.at[slot], in_sem.at[slot, 2]),
         )
 
     for tile in range(2):
@@ -129,37 +111,60 @@
     def table(k):
         return tables[k].reshape(POLES, 8, 128)
 
-    def short_filter(tile, block):
-        t = block * 8
+    power = table(0)
+    for k in range(8):
+        powers[k] = power
+        power = power * table(0)
+
+    def short_filter(tile, t, count):
+        parts = []
         for j in range(3):
-            window = tiles(x.at[tile, j], t + 2, 14)
+            window = tiles(x.at[tile, j], t + 2, count + 6)
             weight = tiles(taps.at[tile, j], 0, TAPS)
-            part = weight[0][None] * window[6:14]
+            part = weight[0][None] * window[6 : 6 + count]
             for i in range(1, TAPS):
-                part = part + weight[i][None] * window[6 - i : 14 - i]
+                part = part + weight[i][None] * window[6 - i : 6 - i + count]
             put_tiles(mix.at[tile, j], t, part)
+            parts.append(part)
+        return total(tiles(c.at[tile], t, count) * parts[0] * (parts[1] * parts[2]))
 
     def load_tile(tile):
         slot = lax.rem(tile, 2)
         for copy in fetch(tile):
             copy.wait()
-        lanes = pl.ds(pl.multiple_of(tile * WIDE, WIDE), WIDE)
         for j in range(3):
-            spread_rows(ins.at[slot, j], x.at[tile, j], HALO)
-            spread(filt[j, :, lanes], taps.at[tile, j], 0)
-        spread_rows(ins.at[slot, 3], c.at[tile], 0)
+            spread(fins[slot, j], taps.at[tile, j], 0)
+
+        def take(block):
+            begin = pl.multiple_of(block * 16, 16)
+            for j in range(3):
+                spread(ins[slot, j, pl.ds(begin, 16), :].astype(F32), x.at[tile, j], HALO + begin)
+            spread(ins[slot, 3, pl.ds(begin, 16), :].astype(F32), c.at[tile], begin)
+
+        def inner(block, acc):
+            acc = acc + short_filter(tile, block * 16 - 24, 16)
+            take(block)
+            return acc
+
+        take(0)
+        take(1)
+        acc = lax.fori_loop(2, ROWS // 16, inner, jnp.zeros((8, 128), F32))
 
         @pl.when(tile < TILES - 2)
         def _():
             for copy in fetch(tile + 2):
                 copy.start()
 
-        def inner(block, _):
-            short_filter(tile, block)
-            return 0
-
-        lax.fori_loop(1, ROWS // 8, inner, 0)
-
+        acc = acc + short_filter(tile, ROWS - 24, 16)
+        acc = acc + short_filter(tile, ROWS - 8, 8)
+        gr[tile, pl.ds(21 * 8, 8), :] = acc
+        gr[tile, pl.ds(22 * 8, (GRADS - 22) * 8), :] = jnp.zeros(((GRADS - 22) * 8, 128), F32)
+
+    def load_loop(tile, _):
+        load_tile(tile)
+        return 0
+
+    lax.fori_loop(0, EARLY, load_loop, 0)
     pl.semaphore_wait(barrier, CHIPS - 1 + 3 + LINES - 1)
     last, first = pl.ds(ROWS - HALO, HALO), pl.ds(0, HALO)
     halo = (
@@ -169,12 +174,7 @@
     )
     for copy in halo:
         copy.start()
-
-    def load_loop(tile, _):
-        load_tile(tile)
-        return 0
-
-    lax.fori_loop(0, TILES, load_loop, 0)
+    lax.fori_loop(EARLY, TILES, load_loop, 0)
     for copy in halo:
         copy.wait()
 
@@ -241,15 +241,15 @@
         d = table(2)
         fwd, bwd = st_enter[g, :, 0], st_enter[g, :, 1]
         fwd_hi, bwd_lo = d * fwd + lo[0], d * bwd + hi[1]
-        ea[0, :, mine(g), :] = jnp.where(low, fwd, fwd_hi)
-        ea[1, :, mine(g), :] = jnp.where(low, bwd_lo, bwd)
+        st[0, :, mine(g), :] = jnp.where(low, fwd, fwd_hi)
+        st[1, :, mine(g), :] = jnp.where(low, bwd_lo, bwd)
         st_give[g, 0] = jnp.where(low, fwd_hi, fwd)
         st_give[g, 1] = jnp.where(low, bwd, bwd_lo)
         st_back_copy(g).start()
 
     def st_5(g):
         st_back_copy(g).wait()
-        ea[:, :, theirs(g), :] = st_land[g]
+        st[:, :, theirs(g), :] = st_land[g]
 
     def st_hooks(slot):
         step = lax.div(slot, 2)
@@ -269,6 +269,8 @@
 
     def local_scan(tile):
         q, k, v = mix.at[tile, 0], mix.at[tile, 1], mix.at[tile, 2]
+        rows = pl.ds(pl.multiple_of(tile * 8, 8), 8)
+        gain = skip[rows, :][None]
 
         def step(block, carry):
             s, b = carry
@@ -282,13 +284,12 @@
                 b = a * b + gf[3 - u][None]
                 fwd.append(total(r * s))
                 bwd.append(total(r * b))
-            put_tiles(yf.at[tile], begin, jnp.stack(fwd))
-            put_tiles(yb.at[tile], end, jnp.stack(bwd[::-1]))
+            put_tiles(yf.at[tile], begin, jnp.stack(fwd) + gain * g)
+            put_tiles(yb.at[tile], end, jnp.stack(bwd[::-1]) + gain * gf)
             return s, b
 
         zero = jnp.zeros((POLES, 8, 128), F32)
         s, b = lax.fori_loop(0, ROWS // 4, step, (zero, zero))
-        rows = pl.ds(pl.multiple_of(tile * 8, 8), 8)
         st[0, :, rows, :] = s
         st[1, :, rows, :] = b
         lax.fori_loop(ROWS // 4, EXT // 4, step, (s, b))
@@ -300,11 +301,8 @@
             spread(nextp[j, :, lanes].astype(F32) * has_next, x.at[tile, j], HALO + ROWS)
         spread(nextc[:, lanes].astype(F32) * has_next, c.at[tile], ROWS)
 
-        def edge(block, _):
-            short_filter(tile, block * (ROWS // 8))
-            return 0
-
-        lax.fori_loop(0, 2, edge, 0)
+        gr[tile, pl.ds(21 * 8, 8), :] += short_filter(tile, 0, 8)
+        short_filter(tile, ROWS, 8)
         local_scan(tile)
 
         @pl.when(lax.rem(tile, 2) == 1)
@@ -372,47 +370,33 @@
         gr[others(h)] = gr_land[h].reshape(half, GRADS * 8, 128)
 
     def correct(tile):
-        q, k, v = mix.at[tile, 0], mix.at[tile, 1], mix.at[tile, 2]
+        q, k_ref, v = mix.at[tile, 0], mix.at[tile, 1], mix.at[tile, 2]
         rows = pl.ds(pl.multiple_of(tile * 8, 8), 8)
-        gain = skip[rows, :][None]
-
-        def ahead(block, carry):
-            e, acc = carry
-            t = block * 4
-            a = table(0)
-            more = []
-            for _ in range(4):
-                e = a * e
-                more.append(total(e))
-            g = tiles(k, t, 4) * tiles(v, t, 4)
-            query, upstream = tiles(q, t, 4), tiles(c.at[tile], t, 4)
-            filtered = tiles(yf.at[tile], t, 4) + jnp.stack(more) + gain * g
-            gf = upstream * query
-            put_tiles(yf.at[tile], t, query * filtered)
-            put_tiles(c.at[tile], t, upstream * filtered)
-            put_tiles(q, t, gf)
-            return e, acc + total(gf * g)
-
-        start = table(1) * ea[0, :, rows, :]
-        e, acc = lax.fori_loop(0, ROWS // 4, ahead, (start, jnp.zeros((8, 128), F32)))
-        gr[tile, pl.ds(21 * 8, 8), :] = acc
-        gr[tile, pl.ds(22 * 8, 16), :] = jnp.zeros((16, 128), F32)
-        lax.fori_loop(ROWS // 4, EXT // 4, ahead, (e, acc))
-
-        def behind(block, e):
-            t = EXT - 4 - block * 4
-            a = table(0)
-            more = []
-            for _ in range(4):
-                e = a * e
-                more.append(total(e))
-            grad_gated = tiles(yb.at[tile], t, 4) + jnp.stack(more[::-1]) + gain * tiles(q, t, 4)
-            key, value = tiles(k, t, 4), tiles(v, t, 4)
-            put_tiles(k, t, grad_gated * value)
-            put_tiles(v, t, grad_gated * key)
-            return e
-
-        lax.fori_loop(0, EXT // 4, behind, table(1) * ea[1, :, rows, :])
+
+        def step(block, carry):
+            e, b = carry
+            begin, end = block * 8, EXT - 8 - block * 8
+            ahead, behind = [], []
+            for k in range(8):
+                fwd, bwd = 0, 0
+                for n in range(0, POLES, 4):
+                    weight = powers[k, n : n + 4]
+                    fwd = fwd + weight * e[n : n + 4]
+                    bwd = bwd + weight * b[n : n + 4]
+                ahead.append(total(fwd))
+                behind.append(total(bwd))
+            filtered = tiles(yf.at[tile], begin, 8) + jnp.stack(ahead)
+            grad_gated = tiles(yb.at[tile], end, 8) + jnp.stack(behind[::-1])
+            query, upstream = tiles(q, begin, 8), tiles(c.at[tile], begin, 8)
+            key, value = tiles(k_ref, end, 8), tiles(v, end, 8)
+            put_tiles(yf.at[tile], begin, query * filtered)
+            put_tiles(c.at[tile], begin, upstream * filtered)
+            put_tiles(k_ref, end, grad_gated * value)
+            put_tiles(v, end, grad_gated * key)
+            return powers[7] * e, powers[7] * b
+
+        r = table(1)
+        lax.fori_loop(0, EXT // 8, step, (r * st[0, :, rows, :], r * st[1, :, rows, :]))
 
     def mixed_grad(tile, j):
         return c.at[tile] if j == 0 else mix.at[tile, j]
@@ -421,14 +405,36 @@
         for j in range(3):
 
             def body(block, acc):
-                t = block * 8
-                grad = tiles(mixed_grad(tile, j), t, 8)
-                window = tiles(x.at[tile, j], t + 2, 14)
-                return tuple(acc[i] + total(grad * window[6 - i : 14 - i]) for i in range(TAPS))
-
-            acc = lax.fori_loop(0, ROWS // 8, body, (jnp.zeros((8, 128), F32),) * TAPS)
+                t = block * 16
+                grad = tiles(mixed_grad(tile, j), t, 16)
+                window = tiles(x.at[tile, j], t + 2, 22)
+                return tuple(acc[i] + total(grad * window[6 - i : 22 - i]) for i in range(TAPS))
+
+            acc = lax.fori_loop(0, ROWS // 16, body, (jnp.zeros((8, 128), F32),) * TAPS)
             for i in range(TAPS):
                 gr[tile, pl.ds((j * TAPS + i) * 8, 8), :] = acc[i]
+
+    stages = (gr_1, gr_2, gr_3, gr_4, gr_5, gr_6)
+    plan = {
+        3: ((1, 0),),
+        4: ((2, 0),),
+        6: ((3, 0),),
+        7: ((1, 1), (4, 0)),
+        8: ((2, 1),),
+        11: ((5, 0),),
+        12: ((3, 1),),
+        13: ((6, 0),),
+        15: ((4, 1),),
+    }
+
+    def gr_hooks(tile, offset):
+        for slot, todo in plan.items():
+            if offset <= slot < offset + TILES:
+
+                @pl.when(tile == slot - offset)
+                def _(todo=todo):
+                    for stage, h in todo:
+                        stages[stage - 1](h)
 
     def post_loop(tile, _):
         @pl.when(lax.rem(tile, 2) == 0)
@@ -438,81 +444,57 @@
         correct(tile)
         tap_grads(tile)
         st_hooks(tile + TILES)
-
-        @pl.when(tile == 3)
-        def _():
-            gr_1(0)
-
-        @pl.when(tile == 4)
-        def _():
-            gr_2(0)
-
-        @pl.when(tile == 6)
-        def _():
-            gr_3(0)
-
+        gr_hooks(tile, 0)
         return 0
 
     lax.fori_loop(0, TILES, post_loop, 0)
-    gr_1(1)
-
-    def leave(tile):
-        slot = lax.rem(tile, 2)
-        lanes = pl.ds(pl.multiple_of(tile * WIDE, WIDE), WIDE)
-        return (
-            pltpu.make_async_copy(outs.at[slot, pl.ds(0, 3)], grad_proj.at[:, :, lanes], out_sem.at[slot, 0]),
-            pltpu.make_async_copy(outs.at[slot, 3], output.at[:, lanes], out_sem.at[slot, 1]),
-        )
 
     def out_loop(tile, _):
-        slot = lax.rem(tile, 2)
-
-        @pl.when(tile >= 2)
-        def _():
-            for copy in leave(tile - 2):
-                copy.wait()
+        def filter_rows(j, block):
+            t = block * 16
+            ahead = tiles(mixed_grad(tile, j), t, 22)
+            weight = tiles(taps.at[tile, j], 0, TAPS)
+            part = weight[0][None] * ahead[0:16]
+            for i in range(1, TAPS):
+                part = part + weight[i][None] * ahead[i : i + 16]
+            put_tiles(x.at[tile, j], t, part)
+
+        def give(source, j, block):
+            begin = pl.multiple_of(block * 16, 16)
+            for lane in range(8):
+                value = source[pl.ds(begin * 8 + lane, 16, stride=8), :]
+                lanes = pl.ds(pl.multiple_of(tile * WIDE + lane * 128, 128), 128)
+                outs[j, pl.ds(begin, 16), lanes] = value.astype(BF16)
+
+        def body(block, _):
+            for j in range(3):
+                give(x.at[tile, j], j, block - 1)
+            give(yf.at[tile], 3, block)
+            for j in range(3):
+                filter_rows(j, block)
+            return 0
 
         for j in range(3):
-
-            def body(block, _):
-                t = block * 8
-                ahead = tiles(mixed_grad(tile, j), t, 14)
-                weight = tiles(taps.at[tile, j], 0, TAPS)
-                part = weight[0][None] * ahead[0:8]
-                for i in range(1, TAPS):
-                    part = part + weight[i][None] * ahead[i : i + 8]
-                put_tiles(x.at[tile, j], t, part)
-                return 0
-
-            lax.fori_loop(0, ROWS // 8, body, 0)
-            gather_rows(x.at[tile, j], outs.at[slot, j])
-        gather_rows(yf.at[tile], outs.at[slot, 3])
-        for copy in leave(tile):
-            copy.start()
-
-        @pl.when(tile == 0)
-        def _():
-            gr_4(0)
-            gr_2(1)
-
-        @pl.when(tile == 4)
-        def _():
-            gr_5(0)
-            gr_3(1)
-
-        @pl.when(tile == 6)
-        def _():
-            gr_6(0)
-
+            filter_rows(j, 0)
+        give(yf.at[tile], 3, 0)
+        lax.fori_loop(1, ROWS // 16, body, 0)
+        for j in range(3):
+            give(x.at[tile, j], j, ROWS // 16 - 1)
+
+        gr_hooks(tile, TILES)
         return 0
 
     lax.fori_loop(0, TILES, out_loop, 0)
-    gr_4(1)
     gr_5(1)
-    for tile in range(TILES - 2, TILES):
-        for copy in leave(tile):
-            copy.wait()
     gr_6(1)
+
+
+def leave_kernel(outs, gr, output, grad_proj, grad_short, grad_skip, sem):
+    copies = [
+        pltpu.make_async_copy(outs.at[j], grad_proj.at[j], sem.at[j]) for j in range(3)
+    ] + [pltpu.make_async_copy(outs.at[3], output, sem.at[3])]
+    for copy in copies:
+        copy.start()
     for tile in range(TILES):
         grad_skip[tile * 8 : tile * 8 + 8, :] = gr[tile, 21 * 8 : 22 * 8, :]
         for j in range(3):
@@ -520,30 +502,53 @@
                 value = gr[tile, pl.ds(j * TAPS * 8 + lane, TAPS, stride=8), :]
                 begin = tile * WIDE + lane * 128
                 grad_short[j, :, begin : begin + 128] = value
-
-
-def whole(proj, cot, filt, skip, rates, weights):
-    channels = proj.shape[2]
+    for copy in copies:
+        copy.wait()
+
+
+def leave(outs, gr):
+    channels = outs.shape[2]
     anywhere = pl.BlockSpec(memory_space=pl.ANY)
     vmem = pl.BlockSpec(memory_space=pltpu.VMEM)
-
-    def buffer(*shape, kind=F32):
-        return pltpu.VMEM(shape, kind)
-
-    def dma(*shape):
-        return pltpu.SemaphoreType.DMA(shape)
-
     return pl.pallas_call(
-        kernel,
-        name="hyena",
+        leave_kernel,
+        name="leave",
         out_shape=(
             jax.ShapeDtypeStruct((ROWS, channels), BF16),
             jax.ShapeDtypeStruct((3, ROWS, channels), BF16),
             jax.ShapeDtypeStruct((3, TAPS, channels), F32),
             jax.ShapeDtypeStruct((TILES * 8, 128), F32),
         ),
-        in_specs=[anywhere, anywhere, vmem, vmem, vmem, vmem],
+        in_specs=[vmem, vmem],
         out_specs=(anywhere, anywhere, vmem, vmem),
+        scratch_shapes=[pltpu.SemaphoreType.DMA((4,))],
+        compiler_params=pltpu.CompilerParams(vmem_limit_bytes=4 << 20),
+    )(
+        pltpu.with_memory_space_constraint(outs, pltpu.VMEM),
+        pltpu.with_memory_space_constraint(gr, pltpu.VMEM),
+    )
+
+
+def whole(proj, cot, filt, skip, rates, weights):
+    channels = proj.shape[2]
+    anywhere = pl.BlockSpec(memory_space=pl.ANY)
+    vmem = pl.BlockSpec(memory_space=pltpu.VMEM)
+
+    def buffer(*shape, kind=F32):
+        return pltpu.VMEM(shape, kind)
+
+    def dma(*shape):
+        return pltpu.SemaphoreType.DMA(shape)
+
+    return pl.pallas_call(
+        kernel,
+        name="hyena",
+        out_shape=(
+            buffer(4, ROWS, channels, kind=BF16),
+            buffer(TILES, GRADS * 8, 128),
+        ),
+        in_specs=[anywhere, anywhere, anywhere, vmem, vmem, vmem],
+        out_specs=(vmem, vmem),
         scratch_shapes=[
             buffer(TILES, 3, (EXT + HALO) * 8, 128),
             buffer(TILES, 3, EXT * 8, 128),
@@ -551,12 +556,13 @@
             buffer(TILES, EXT * 8, 128),
             buffer(TILES, EXT * 8, 128),
             buffer(2, 4, ROWS, WIDE, kind=BF16),
-            buffer(2, 4, ROWS, WIDE, kind=BF16),
+            buffer(2, 3, TAPS, WIDE),
             buffer(3, HALO, channels, kind=BF16),
             buffer(3, HALO, channels, kind=BF16),
             buffer(HALO, channels, kind=BF16),
             buffer(TILES, 3, TAPS * 8, 128),
             buffer(4, POLES * 8, 128),
+            buffer(8, POLES, 8, 128),
             buffer(2, POLES, TILES * 8, 128),
             buffer(GROUPS, 2, POLES, 8, 128),
             buffer(GROUPS, CHIPS, 2, 8, 128),
@@ -565,8 +571,6 @@
             buffer(GROUPS, CHIPS, 2, 8, 128),
             buffer(GROUPS, 2, POLES, 8, 128),
             buffer(GROUPS, 2, POLES, 8, 128),
-            buffer(2, POLES, TILES * 8, 128),
-            buffer(TILES, GRADS * 8, 128),
             buffer(SUMS, TILES // SUMS // 2, GRADS * 8, 128),
             buffer(SUMS, CHIPS, PIECE, 128),
             buffer(SUMS, CHIPS, PIECE, 128),
@@ -575,8 +579,7 @@
             buffer(SUMS, LINES, PIECE, 128),
             buffer(SUMS, CHIPS, PIECE, 128),
             buffer(SUMS, CHIPS, PIECE, 128),
-            dma(2, 2),
-            dma(2, 2),
+            dma(2, 3),
             dma(3),
             dma(3),
         ]
@@ -585,7 +588,7 @@
         + [dma(SUMS)] * 4
         + [dma(SUMS, LINES)] * 2,
         compiler_params=pltpu.CompilerParams(
-            collective_id=0, has_side_effects=True, vmem_limit_bytes=60 << 20
+            collective_id=0, has_side_effects=True, vmem_limit_bytes=52 << 20
         ),
     )(proj, cot, filt, skip, rates, weights)
 
@@ -593,9 +596,8 @@
 def local(projected, short_filter, residues, decay_rates, skip_gain, cotangent):
     proj = jnp.transpose(projected[0], (1, 0, 2))
     skip = skip_gain.reshape(TILES * 8, 128)
-    output, grad_proj, grad_short, grad_skip = whole(
-        proj, cotangent[0], short_filter, skip, decay_rates.T, residues.T
-    )
+    outs, grads = whole(proj, cotangent[0], short_filter, skip, decay_rates.T, residues.T)
+    output, grad_proj, grad_short, grad_skip = leave(outs, grads)
     return (
         output[None],
         jnp.transpose(grad_proj, (1, 0, 2))[None],

time: 102 us -> 89.8 us (0.88)
  local copies, waits for them, and re-layouts: 10.9 us -> 0 us
  Pallas kernels: 90 us -> 88.8 us
    unnamed x8 -> x0, local copies, waits for them, and re-layouts: 10.9 us -> none
    pallas_call x1 -> x2, Pallas kernels: 90 us -> 88.8 us  [the longest x1 84.6 us: whole(): pl.pallas_call(kernel, name='hyena', out_shape=(buffer(4, ROWS, channels,...]
where the time goes in v3:
time: 89.8 us; the launch traced here: 89.5 us
  Pallas kernels  88.8 us (99%)
    pallas_call x1, Pallas kernels, whole(): pl.pallas_call(kernel, name='hyena', out_shape=(buffer(4, ROWS, channels,...  84.6 us
    pallas_call x1, Pallas kernels, leave(): pl.pallas_call(leave_kernel, name='leave', out_shape=(jax.ShapeDtypeStruc...  4.25 us

profile of v3, /device:TPU:1, one launch (start us, length us, event | category | flops | bytes accessed | tf_op | source)
XLA Modules:
  0.0 89.5 jit_solution(11220124825261469307)
XLA Ops:
  0.6 84.6 %hyena.1 = (bf16[4,128,8192]{2,1,0:T(8,128)(2,1)S(1)}, f32[8,192,128]{2,1,0:T(8,128)S(1)}) custom-call(bf16[3,128,8192]{2,1,0:T(8,128)(2,1)} %bitcast.12, bf16[128,8192]{1,0:T(8,128)(2,1)} %bitcast.13, f32[3,7,8192]{2,1,0:T(8,128)} %filt.1, f32[64,128]{1,0:T(8,128)} %bitcast.14, f32[16,512]{1,0:T(8,128)} %bitcast.15, f32[16,512]{1,0:T(8,128)} %bitcast.16), custom_call_target="tpu_custom_call" | custom-call | tf_op jit(solution)/shard_map/hyena/pallas_call | solution.py:543
  85.2 4.2 %leave.1 = (bf16[128,8192]{1,0:T(8,128)(2,1)}, bf16[3,128,8192]{2,1,0:T(8,128)(2,1)}, f32[3,7,8192]{2,1,0:T(8,128)}, f32[64,128]{1,0:T(8,128)}) custom-call(bf16[4,128,8192]{2,1,0:T(8,128)(2,1)S(1)} %get-tuple-element.10.outs, f32[8,192,128]{2,1,0:T(8,128)S(1)} %get-tuple-element.11.gr), custom_call_target="tpu_custom_call" | custom-call | tf_op jit(solution)/shard_map/leave/pallas_call | solution.py:513

commit v4 on v3

--- a/solution.py
+++ b/solution.py
@@ -17,11 +17,12 @@
 TAPS = 7
 CHIPS = 16
 LINES = 4
-GRADS = 24
+GRADS = 32
 GROUPS = 4
-SUMS = 2
+SUMS = ((0, 4, 24), (4, 2, 32), (6, 2, 32))
+FAR = (10, 6, 14, 9, 11, 2, 8, 5, 7, 13, 15, 1, 3, 4, 12)
 EARLY = 2
-PIECE = TILES // SUMS // 2 * GRADS * 8 // CHIPS
+PIECES = tuple(many // 2 * rows * 8 // CHIPS for _, many, rows in SUMS)
 
 
 def spread(value, target, row):
@@ -184,7 +185,8 @@
             remote(source(other), target.at[chip], send_sem, recv_sem, dp, other * 2 + core).start()
             return 0
 
-        lax.fori_loop(1, CHIPS, start, 0)
+        for offset in FAR:
+            start(offset, 0)
         target[chip] = source(chip)[...]
 
     def plane_wait(target, send_sem, recv_sem):
@@ -255,17 +257,17 @@
         step = lax.div(slot, 2)
         even = lax.rem(slot, 2) == 0
 
+        @pl.when(jnp.logical_and(even, jnp.logical_and(step >= 1, step < GROUPS + 1)))
+        def _():
+            st_2(step - 1)
+
+        @pl.when(jnp.logical_and(even, jnp.logical_and(step >= 2, step < GROUPS + 2)))
+        def _():
+            st_3(step - 2)
+
         @pl.when(jnp.logical_and(even, jnp.logical_and(step >= 3, step < GROUPS + 3)))
         def _():
             st_4(step - 3)
-
-        @pl.when(jnp.logical_and(even, jnp.logical_and(step >= 2, step < GROUPS + 2)))
-        def _():
-            st_3(step - 2)
-
-        @pl.when(jnp.logical_and(even, jnp.logical_and(step >= 1, step < GROUPS + 1)))
-        def _():
-            st_2(step - 1)
 
     def local_scan(tile):
         q, k, v = mix.at[tile, 0], mix.at[tile, 1], mix.at[tile, 2]
@@ -314,38 +316,36 @@
 
     lax.fori_loop(0, TILES, scan_loop, 0)
 
-    half = TILES // SUMS // 2
-
-    def own(h):
-        return pl.ds(h * 2 * half + core * half, half)
-
-    def others(h):
-        return pl.ds(h * 2 * half + (1 - core) * half, half)
+    def gr_half(h, which):
+        begin, many, rows = SUMS[h]
+        half = many // 2
+        return gr.at[pl.ds(begin + which * half, half), pl.ds(0, rows * 8), :]
 
     def gr_pair_copy(h):
-        return remote(gr.at[others(h)], gr_pair.at[h], gr_ps.at[h, 0], gr_pr.at[h, 0], dp, pair)
+        return remote(gr_half(h, 1 - core), gr_pair[h], gr_ps.at[h, 0], gr_pr.at[h, 0], dp, pair)
 
     def gr_back_copy(h):
-        return remote(gr_around.at[h], gr_land.at[h], gr_ps.at[h, 1], gr_pr.at[h, 1], dp, pair)
+        return remote(gr_around[h], gr_land[h], gr_ps.at[h, 1], gr_pr.at[h, 1], dp, pair)
 
     def gr_1(h):
         gr_pair_copy(h).start()
 
     def gr_2(h):
         gr_pair_copy(h).wait()
-        gr_cut[h] = (gr[own(h)] + gr_pair[h]).reshape(CHIPS, PIECE, 128)
-        plane_send(lambda q: gr_cut.at[h, q], gr_came.at[h], gr_s1.at[h], gr_r1.at[h])
+        both = gr_half(h, core)[...] + gr_pair[h][...]
+        gr_cut[h][...] = both.reshape(CHIPS, PIECES[h], 128)
+        plane_send(lambda q: gr_cut[h].at[q], gr_came[h], gr_s1.at[h], gr_r1.at[h])
 
     def line_copy(h, other, slot):
-        return remote(gr_part.at[h], gr_lines.at[h, slot], gr_ls.at[h, other], gr_lr.at[h, slot], other, me)
+        return remote(gr_part[h], gr_lines[h].at[slot], gr_ls.at[h, other], gr_lr.at[h, slot], other, me)
 
     def gr_3(h):
-        plane_wait(gr_came.at[h], gr_s1.at[h], gr_r1.at[h])
-        part = gr_came[h, 0]
+        plane_wait(gr_came[h], gr_s1.at[h], gr_r1.at[h])
+        part = gr_came[h][0]
         for q in range(1, CHIPS):
-            part = part + gr_came[h, q]
-        gr_part[h] = part
-        gr_lines[h, dp] = part
+            part = part + gr_came[h][q]
+        gr_part[h][...] = part
+        gr_lines[h][dp] = part
         for offset in range(1, LINES):
             line_copy(h, lax.rem(dp + offset, LINES), dp).start()
 
@@ -354,20 +354,21 @@
             other = lax.rem(dp + offset, LINES)
             line_copy(h, other, other).wait_recv()
             line_copy(h, other, dp).wait_send()
-        part = gr_lines[h, 0]
+        part = gr_lines[h][0]
         for q in range(1, LINES):
-            part = part + gr_lines[h, q]
-        gr_whole[h] = part
-        plane_send(lambda q: gr_whole.at[h], gr_around.at[h], gr_s2.at[h], gr_r2.at[h])
+            part = part + gr_lines[h][q]
+        gr_whole[h][...] = part
+        plane_send(lambda q: gr_whole[h], gr_around[h], gr_s2.at[h], gr_r2.at[h])
 
     def gr_5(h):
-        plane_wait(gr_around.at[h], gr_s2.at[h], gr_r2.at[h])
+        plane_wait(gr_around[h], gr_s2.at[h], gr_r2.at[h])
         gr_back_copy(h).start()
 
     def gr_6(h):
         gr_back_copy(h).wait()
-        gr[own(h)] = gr_around[h].reshape(half, GRADS * 8, 128)
-        gr[others(h)] = gr_land[h].reshape(half, GRADS * 8, 128)
+        _, many, rows = SUMS[h]
+        gr_half(h, core)[...] = gr_around[h][...].reshape(many // 2, rows * 8, 128)
+        gr_half(h, 1 - core)[...] = gr_land[h][...].reshape(many // 2, rows * 8, 128)
 
     def correct(tile):
         q, k_ref, v = mix.at[tile, 0], mix.at[tile, 1], mix.at[tile, 2]
@@ -417,14 +418,15 @@
     stages = (gr_1, gr_2, gr_3, gr_4, gr_5, gr_6)
     plan = {
         3: ((1, 0),),
-        4: ((2, 0),),
-        6: ((3, 0),),
-        7: ((1, 1), (4, 0)),
-        8: ((2, 1),),
-        11: ((5, 0),),
-        12: ((3, 1),),
-        13: ((6, 0),),
-        15: ((4, 1),),
+        5: ((2, 0), (1, 1)),
+        6: ((2, 1),),
+        7: ((1, 2), (3, 0)),
+        8: ((2, 2), (3, 1)),
+        9: ((4, 0),),
+        11: ((4, 1),),
+        12: ((3, 2),),
+        13: ((5, 0),),
+        15: ((4, 2), (6, 0), (5, 1)),
     }
 
     def gr_hooks(tile, offset):
@@ -485,8 +487,9 @@
         return 0
 
     lax.fori_loop(0, TILES, out_loop, 0)
-    gr_5(1)
     gr_6(1)
+    gr_5(2)
+    gr_6(2)
 
 
 def leave_kernel(outs, gr, output, grad_proj, grad_short, grad_skip, sem):
@@ -540,6 +543,8 @@
     def dma(*shape):
         return pltpu.SemaphoreType.DMA(shape)
 
+    slots = tuple(buffer(CHIPS, piece, 128) for piece in PIECES)
+    pieces = tuple(buffer(piece, 128) for piece in PIECES)
     return pl.pallas_call(
         kernel,
         name="hyena",
@@ -571,22 +576,22 @@
             buffer(GROUPS, CHIPS, 2, 8, 128),
             buffer(GROUPS, 2, POLES, 8, 128),
             buffer(GROUPS, 2, POLES, 8, 128),
-            buffer(SUMS, TILES // SUMS // 2, GRADS * 8, 128),
-            buffer(SUMS, CHIPS, PIECE, 128),
-            buffer(SUMS, CHIPS, PIECE, 128),
-            buffer(SUMS, PIECE, 128),
-            buffer(SUMS, PIECE, 128),
-            buffer(SUMS, LINES, PIECE, 128),
-            buffer(SUMS, CHIPS, PIECE, 128),
-            buffer(SUMS, CHIPS, PIECE, 128),
+            tuple(buffer(many // 2, rows * 8, 128) for _, many, rows in SUMS),
+            slots,
+            slots,
+            pieces,
+            pieces,
+            tuple(buffer(LINES, piece, 128) for piece in PIECES),
+            slots,
+            slots,
             dma(2, 3),
             dma(3),
             dma(3),
         ]
         + [dma(GROUPS)] * 8
-        + [dma(SUMS, 2)] * 2
-        + [dma(SUMS)] * 4
-        + [dma(SUMS, LINES)] * 2,
+        + [dma(len(SUMS), 2)] * 2
+        + [dma(len(SUMS))] * 4
+        + [dma(len(SUMS), LINES)] * 2,
         compiler_params=pltpu.CompilerParams(
             collective_id=0, has_side_effects=True, vmem_limit_bytes=52 << 20
         ),

time: 89.8 us -> 87.7 us (0.977)
  Pallas kernels: 88.8 us -> 86.8 us
    pallas_call x1, Pallas kernels: 84.6 us -> 82.5 us  [whole(): pl.pallas_call(kernel, name='hyena', out_shape=(buffer(4, ROWS, channels,...]
where the time goes in v4:
time: 87.7 us; the launch traced here: 87.4 us
  Pallas kernels  86.8 us (99%)
    pallas_call x1, Pallas kernels, whole(): pl.pallas_call(kernel, name='hyena', out_shape=(buffer(4, ROWS, channels,...  82.5 us
    pallas_call x1, Pallas kernels, leave(): pl.pallas_call(leave_kernel, name='leave', out_shape=(jax.ShapeDtypeStruc...  4.25 us

profile of v4, /device:TPU:1, one launch (start us, length us, event | category | flops | bytes accessed | tf_op | source)
XLA Modules:
  0.0 87.4 jit_solution(16296021688422051284)
XLA Ops:
  0.6 82.5 %hyena.1 = (bf16[4,128,8192]{2,1,0:T(8,128)(2,1)S(1)}, f32[8,256,128]{2,1,0:T(8,128)S(1)}) custom-call(bf16[3,128,8192]{2,1,0:T(8,128)(2,1)} %bitcast.12, bf16[128,8192]{1,0:T(8,128)(2,1)} %bitcast.13, f32[3,7,8192]{2,1,0:T(8,128)} %filt.1, f32[64,128]{1,0:T(8,128)} %bitcast.14, f32[16,512]{1,0:T(8,128)} %bitcast.15, f32[16,512]{1,0:T(8,128)} %bitcast.16), custom_call_target="tpu_custom_call" | custom-call | tf_op jit(solution)/shard_map/hyena/pallas_call | solution.py:548
  83.2 4.2 %leave.1 = (bf16[128,8192]{1,0:T(8,128)(2,1)}, bf16[3,128,8192]{2,1,0:T(8,128)(2,1)}, f32[3,7,8192]{2,1,0:T(8,128)}, f32[64,128]{1,0:T(8,128)}) custom-call(bf16[4,128,8192]{2,1,0:T(8,128)(2,1)S(1)} %get-tuple-element.10.outs, f32[8,256,128]{2,1,0:T(8,128)S(1)} %get-tuple-element.11.gr), custom_call_target="tpu_custom_call" | custom-call | tf_op jit(solution)/shard_map/leave/pallas_call | solution.py:516

commit v5 on v4

--- a/solution.py
+++ b/solution.py
@@ -74,20 +74,6 @@
             device_id_type=MESH,
         )
 
-    barrier = pltpu.get_barrier_semaphore()
-
-    def greet(offset, _):
-        other = lax.rem(chip + offset, CHIPS) * 2 + core
-        pl.semaphore_signal(barrier, inc=1, device_id=(dp, other), device_id_type=MESH)
-        return 0
-
-    lax.fori_loop(1, CHIPS, greet, 0)
-    for other in (chip * 2 + 1 - core, up, down):
-        pl.semaphore_signal(barrier, inc=1, device_id=(dp, other), device_id_type=MESH)
-    for offset in range(1, LINES):
-        line = lax.rem(dp + offset, LINES)
-        pl.semaphore_signal(barrier, inc=1, device_id=(line, me), device_id_type=MESH)
-
     def fetch(tile):
         slot = lax.rem(tile, 2)
         lanes = pl.ds(pl.multiple_of(tile * WIDE, WIDE), WIDE)
@@ -100,6 +86,20 @@
     for tile in range(2):
         for copy in fetch(tile):
             copy.start()
+
+    barrier = pltpu.get_barrier_semaphore()
+
+    def greet(offset, _):
+        other = lax.rem(chip + offset, CHIPS) * 2 + core
+        pl.semaphore_signal(barrier, inc=1, device_id=(dp, other), device_id_type=MESH)
+        return 0
+
+    lax.fori_loop(1, CHIPS, greet, 0)
+    for other in (chip * 2 + 1 - core, up, down):
+        pl.semaphore_signal(barrier, inc=1, device_id=(dp, other), device_id_type=MESH)
+    for offset in range(1, LINES):
+        line = lax.rem(dp + offset, LINES)
+        pl.semaphore_signal(barrier, inc=1, device_id=(line, me), device_id_type=MESH)
 
     for quarter in range(4):
         lanes = slice(quarter * 128, (quarter + 1) * 128)
@@ -276,14 +276,14 @@
 
         def step(block, carry):
             s, b = carry
-            begin, end = block * 4, EXT - 4 - block * 4
+            begin, end = block * 8, EXT - 8 - block * 8
             a, r = table(0), table(1)
-            g = tiles(k, begin, 4) * tiles(v, begin, 4)
-            gf = tiles(c.at[tile], end, 4) * tiles(q, end, 4)
+            g = tiles(k, begin, 8) * tiles(v, begin, 8)
+            gf = tiles(c.at[tile], end, 8) * tiles(q, end, 8)
             fwd, bwd = [], []
-            for u in range(4):
+            for u in range(8):
                 s = a * s + g[u][None]
-                b = a * b + gf[3 - u][None]
+                b = a * b + gf[7 - u][None]
                 fwd.append(total(r * s))
                 bwd.append(total(r * b))
             put_tiles(yf.at[tile], begin, jnp.stack(fwd) + gain * g)
@@ -291,10 +291,10 @@
             return s, b
 
         zero = jnp.zeros((POLES, 8, 128), F32)
-        s, b = lax.fori_loop(0, ROWS // 4, step, (zero, zero))
+        s, b = lax.fori_loop(0, ROWS // 8, step, (zero, zero))
         st[0, :, rows, :] = s
         st[1, :, rows, :] = b
-        lax.fori_loop(ROWS // 4, EXT // 4, step, (s, b))
+        lax.fori_loop(ROWS // 8, EXT // 8, step, (s, b))
 
     def scan_loop(tile, _):
         lanes = pl.ds(pl.multiple_of(tile * WIDE, WIDE), WIDE)

time: 87.7 us -> 87.2 us (level)
  no operation moved by 1% of the time
where the time goes in v5:
time: 87.2 us; the launch traced here: 86.9 us
  Pallas kernels  86.3 us (99%)
    pallas_call x1, Pallas kernels, whole(): pl.pallas_call(kernel, name='hyena', out_shape=(buffer(4, ROWS, channels,...  82.1 us
    pallas_call x1, Pallas kernels, leave(): pl.pallas_call(leave_kernel, name='leave', out_shape=(jax.ShapeDtypeStruc...  4.25 us

profile of v5, /device:TPU:1, one launch (start us, length us, event | category | flops | bytes accessed | tf_op | source)
XLA Modules:
  0.0 86.9 jit_solution(3347603903709960613)
XLA Ops:
  0.6 82.1 %hyena.1 = (bf16[4,128,8192]{2,1,0:T(8,128)(2,1)S(1)}, f32[8,256,128]{2,1,0:T(8,128)S(1)}) custom-call(bf16[3,128,8192]{2,1,0:T(8,128)(2,1)} %bitcast.12, bf16[128,8192]{1,0:T(8,128)(2,1)} %bitcast.13, f32[3,7,8192]{2,1,0:T(8,128)} %filt.1, f32[64,128]{1,0:T(8,128)} %bitcast.14, f32[16,512]{1,0:T(8,128)} %bitcast.15, f32[16,512]{1,0:T(8,128)} %bitcast.16), custom_call_target="tpu_custom_call" | custom-call | tf_op jit(solution)/shard_map/hyena/pallas_call | solution.py:548
  82.7 4.2 %leave.1 = (bf16[128,8192]{1,0:T(8,128)(2,1)}, bf16[3,128,8192]{2,1,0:T(8,128)(2,1)}, f32[3,7,8192]{2,1,0:T(8,128)}, f32[64,128]{1,0:T(8,128)}) custom-call(bf16[4,128,8192]{2,1,0:T(8,128)(2,1)S(1)} %get-tuple-element.10.outs, f32[8,256,128]{2,1,0:T(8,128)S(1)} %get-tuple-element.11.gr), custom_call_target="tpu_custom_call" | custom-call | tf_op jit(solution)/shard_map/leave/pallas_call | solution.py:516
